TPU v7x, 128 devices: a whole 4x4x4 slice. The times are simulated.
128 devices in a mesh: hid: 16 (over x, y), wid: 4 (over z_lo, core), rep: 2 (over z_hi).
Axes of the slice: x: 4, y: 4, z: 4 (z_hi: 2, z_lo: 2; z = z_hi * 2 + z_lo), core: 2. Of those that a mesh axis runs over, the one named last changes fastest.
Arguments:
- grad_out: bfloat16 [2, 1024, 8192], P('rep', None, 'wid'), may hold values from -6 to 6
- down_weight: bfloat16 [28672, 8192], P('hid', 'wid'), may hold values from -0.03125 to 0.03125
- saved_gate: bfloat16 [2, 1024, 28672], P('rep', 'wid', 'hid'), may hold values from -6 to 6
- saved_up: bfloat16 [2, 1024, 28672], P('rep', 'wid', 'hid'), may hold values from -6 to 6
- saved_codes: int32 [2, 1024, 28672], P('rep', 'wid', 'hid'), may hold values from -128 to 127, as said below
- exponents: int32 [2, 1024, 224], P('rep', 'wid', 'hid'), may hold values from -12 to -9
Outputs:
- grad_gate: bfloat16 [2, 1024, 28672], P('rep', 'wid', 'hid')
- grad_up: bfloat16 [2, 1024, 28672], P('rep', 'wid', 'hid')
- grad_down: float32 [28672, 8192], P('hid', ('wid', 'rep'))
Inputs may be any that keep to these rules, and one draw needn't show every extreme that they name: `saved_codes`: codes at the clip limits -128 and 127 both occur.
All inputs are finite; a program needn't handle non-finite values.
Results may differ from a plain program's by a relative error of at most 0.014.
Values may be sent and summed in bfloat16 or wider, within the bound.
No kernel may reach another device: no remote copies, remote signals or barrier semaphores. Data moves between devices by JAX's collectives and lax.ppermute only.
A program may use at most 128 MiB of HBM per device.

v0:
```python
import math

import jax
import jax.numpy as jnp
from jax import lax
from jax.sharding import PartitionSpec as P

BLOCK = 128


def from_partner(block, axis, distance):
    count = lax.axis_size(axis)
    route = []
    for low in range(count):
        high = low | 1 << distance
        if high != low and high < count:
            route += [(low, high), (high, low)]
    return lax.ppermute(block, axis, route)


def sylvester(order):
    indices = jnp.arange(order, dtype=jnp.int32)
    both = jnp.bitwise_and(indices[:, None], indices[None, :])
    parity = jnp.zeros((order, order), jnp.int32)
    for bit_index in range(order.bit_length() - 1):
        parity = jnp.bitwise_xor(parity, jnp.bitwise_and(jnp.right_shift(both, bit_index), 1))
    return (1 - 2 * parity).astype(jnp.float32)


def block_transform(values, order):
    tok_local, hidden_local = values.shape
    table_block = sylvester(order) / math.sqrt(order)
    shaped = values.reshape(tok_local, hidden_local // order, order)
    shaped = jnp.einsum("tbk,kj->tbj", shaped, table_block, precision=lax.Precision.HIGHEST)
    return shaped.reshape(tok_local, hidden_local)


def shards(grad_out, down_weight, saved_gate, saved_up, saved_codes, exponents):
    out_rows = grad_out[0]
    codes_local = saved_codes[0]
    tok_local, hidden_local = codes_local.shape
    block_count = hidden_local // BLOCK
    scales = jnp.exp2(exponents[0].astype(jnp.float32))
    dequant = (
        (
            codes_local.astype(jnp.float32).reshape(tok_local, block_count, BLOCK)
            * scales[:, :, None]
        )
        .reshape(tok_local, hidden_local)
        .astype(jnp.bfloat16)
    )
    rows = out_rows
    grad_quant = lax.psum_scatter(
        lax.dot_general(
            rows, down_weight, (((1,), (1,)), ((), ())), preferred_element_type=jnp.float32
        ).astype(jnp.bfloat16),
        "wid",
        scatter_dimension=0,
        tiled=True,
    ).astype(jnp.float32)
    keep_mask = (codes_local > -128) & (codes_local < 127)
    masked = jnp.where(keep_mask, grad_quant, jnp.float32(0.0))
    mixed = block_transform(masked, BLOCK)
    group_count = lax.axis_size("hid")
    position = lax.axis_index("hid")
    for bit_index in range(group_count.bit_length() - 1):
        partner = from_partner(mixed.astype(jnp.bfloat16), "hid", bit_index).astype(mixed.dtype)
        upper = jnp.bitwise_and(jnp.right_shift(position, bit_index), 1) == 1
        mixed = jnp.where(upper, partner - mixed, mixed + partner)
    grad_hidden = mixed * (1.0 / math.sqrt(group_count))
    gate_local = saved_gate[0].astype(jnp.float32)
    up_local = saved_up[0].astype(jnp.float32)
    sigmoid_gate = jax.nn.sigmoid(gate_local)
    grad_gate = (
        grad_hidden * up_local * sigmoid_gate * (1.0 + gate_local * (1.0 - sigmoid_gate))
    ).astype(jnp.bfloat16)
    grad_up = (grad_hidden * gate_local * sigmoid_gate).astype(jnp.bfloat16)
    rows = out_rows
    replica_term = lax.dot_general(
        lax.all_gather(dequant, "wid", axis=0, tiled=True),
        rows,
        (((0,), (0,)), ((), ())),
        preferred_element_type=jnp.float32,
    )
    grad_down = lax.psum_scatter(
        replica_term.astype(jnp.bfloat16), "rep", scatter_dimension=1, tiled=True
    ).astype(jnp.float32)
    return (grad_gate[None], grad_up[None], grad_down)


def solution(mesh):
    in_specs = (
        P("rep", None, "wid"),
        P("hid", "wid"),
        P("rep", "wid", "hid"),
        P("rep", "wid", "hid"),
        P("rep", "wid", "hid"),
        P("rep", "wid", "hid"),
    )
    out_specs = (P("rep", "wid", "hid"), P("rep", "wid", "hid"), P("hid", ("wid", "rep")))
    return jax.shard_map(shards, mesh=mesh, in_specs=in_specs, out_specs=out_specs, check_vma=False)
```

profile of v0, /device:TPU:0, one launch (start us, length us, event | category | flops | bytes accessed | tf_op | source)
XLA Modules:
  0.0 223.2 jit_solution(2910662900731102619)
XLA Ops:
  7.2 1.8 copy.19
  9.1 1.1 fusion.20
  10.3 13.0 %fusion.3 = bf16[1024,1792]{1,0:T(8,128)(2,1)} fusion(bf16[1792,2048]{1,0:T(8,128)(2,1)} %param.7, bf16[1,1024,2048]{2,1,0:T(8,128)(2,1)} %param.6), kind=kOutput, calls=%fused_computation.4 | convolution fusion | flops 7518027776 | bytes 15204352 | tf_op jit(solution)/shard_map/dot_general | solution.py:54
  23.3 31.0 %all-gather.2.cloned.1.call-done = bf16[1024,1792]{0,1:T(8,128)(2,1)} async-done(((bf16[256,1792]{0,1:T(8,128)(2,1)}), bf16[1024,1792]{0,1:T(8,128)(2,1)}) %all-gather.2.cloned.1.call-update) | async-done | bytes 3670032 | tf_op jit(solution)/shard_map/all_gather | solution.py:80
  54.4 12.5 %convolution_convert_fusion = bf16[1792,2048]{1,0:T(8,128)(2,1)} fusion(bf16[1024,1792]{0,1:T(8,128)(2,1)} %all-gather.2.cloned.1.call-done, bf16[1,1024,2048]{2,1,0:T(8,128)(2,1)} %param.6), kind=kOutput, calls=%fused_computation | convolution fusion | flops 7519862784 | bytes 15204352 | tf_op jit(solution)/shard_map/dot_general | solution.py:79
  66.9 32.4 %reduce-scatter.3.cloned.1.call-done = bf16[256,1792]{1,0:T(8,128)(2,1)} async-done(((bf16[1024,1792]{1,0:T(8,128)(2,1)}), bf16[256,1792]{1,0:T(8,128)(2,1)}) %reduce-scatter.3.cloned.1.call-update) | async-done | bytes 917520 | tf_op jit(solution)/shard_map/reduce_scatter | solution.py:53
  99.3 2.7 %convert_select_fusion = f32[256,1792]{1,0:T(8,128)} fusion(bf16[256,1792]{1,0:T(8,128)(2,1)} %reduce-scatter.3.cloned.1.call-done, s32[1,256,1792]{2,1,0:T(8,128)S(1)} %copy-done.1), kind=kLoop, calls=%fused_computation.33 | loop fusion | flops 2293760 | bytes 4587520 | tf_op jit(solution)/shard_map/jit(_where)/select_n | solution.py:62
  102.1 1.8 copy.14
  103.9 3.1 %fusion.25 = f32[256,14,128]{0,2,1:T(8,128)} fusion(f32[256,14,128]{0,2,1:T(8,128)S(1)} %bitcast.43), kind=kOutput, calls=%fused_computation.38 | convolution fusion | flops 705052672 | bytes 3670016 | tf_op jit(solution)/shard_map/tbk,kj->tbj/dot_general | solution.py:34
  107.0 1.8 copy.16
  108.8 1.0 convert_element_type.79
  109.8 1.5 collective-permute-start
  111.3 21.2 %collective-permute-done = bf16[256,1792]{1,0:T(8,128)(2,1)S(1)} collective-permute-done((bf16[256,1792]{1,0:T(8,128)(2,1)}, bf16[256,1792]{1,0:T(8,128)(2,1)S(1)}, u32[]{:S(2)}, u32[]{:S(2)}) %collective-permute-start) | collective-permute-done | bytes 917536 | tf_op jit(solution)/shard_map/ppermute | solution.py:18
  132.4 1.2 fusion.22
  133.6 3.0 %collective-permute-start.1 = (bf16[256,1792]{1,0:T(8,128)(2,1)}, bf16[256,1792]{1,0:T(8,128)(2,1)}, u32[]{:S(2)}, u32[]{:S(2)}) collective-permute-start(bf16[256,1792]{1,0:T(8,128)(2,1)} %fusion.22), channel_id=1, source_target_pairs={{0,16},{16,0},{8,24},{24,8},{32,48},{48,32},{40,56},{56,40},{64,80... | collective-permute-start | bytes 2752520 | tf_op jit(solution)/shard_map/ppermute | solution.py:18
  136.6 20.5 %collective-permute-done.1 = bf16[256,1792]{1,0:T(8,128)(2,1)} collective-permute-done((bf16[256,1792]{1,0:T(8,128)(2,1)}, bf16[256,1792]{1,0:T(8,128)(2,1)}, u32[]{:S(2)}, u32[]{:S(2)}) %collective-permute-start.1) | collective-permute-done | bytes 917536 | tf_op jit(solution)/shard_map/ppermute | solution.py:18
  157.1 3.2 %fusion.70 = (bf16[256,1792]{1,0:T(8,128)(2,1)}, f32[256,1792]{1,0:T(8,128)}) fusion(f32[256,1792]{1,0:T(8,128)S(1)} %copy.16, bf16[256,1792]{1,0:T(8,128)(2,1)S(1)} %collective-permute-done, pred[]{:T(512)S(6)} %eq.15, bf16[256,1792]{1,0:T(8,128)(2,1)} %collective-permute-done.1, pred[]{:T(512)S(6)} %eq.14), kind=kLoop, calls=%fused_computation.85 | loop fusion | flops 4128768 | bytes 6422530 | tf_op jit(solution)/shard_map/convert_element_type | solution.py:67
  160.3 1.5 collective-permute-start.2
  161.8 19.7 %collective-permute-done.2 = bf16[256,1792]{1,0:T(8,128)(2,1)S(1)} collective-permute-done((bf16[256,1792]{1,0:T(8,128)(2,1)}, bf16[256,1792]{1,0:T(8,128)(2,1)S(1)}, u32[]{:S(2)}, u32[]{:S(2)}) %collective-permute-start.2) | collective-permute-done | bytes 917536 | tf_op jit(solution)/shard_map/ppermute | solution.py:18
  181.5 2.8 %fusion.21 = bf16[256,1792]{1,0:T(8,128)(2,1)} fusion(f32[256,1792]{1,0:T(8,128)} %get-tuple-element.4, bf16[256,1792]{1,0:T(8,128)(2,1)S(1)} %collective-permute-done.2, pred[]{:T(512)S(6)} %eq.13), kind=kLoop, calls=%fused_computation.34 | loop fusion | flops 2293760 | bytes 3670017 | tf_op jit(solution)/shard_map/convert_element_type | solution.py:67
  184.3 3.0 %collective-permute-start.3 = (bf16[256,1792]{1,0:T(8,128)(2,1)}, bf16[256,1792]{1,0:T(8,128)(2,1)}, u32[]{:S(2)}, u32[]{:S(2)}) collective-permute-start(bf16[256,1792]{1,0:T(8,128)(2,1)} %fusion.21), channel_id=1, source_target_pairs={{0,64},{64,0},{8,72},{72,8},{16,80},{80,16},{24,88},{88,24},{32,96... | collective-permute-start | bytes 2752520 | tf_op jit(solution)/shard_map/ppermute | solution.py:18
  187.3 19.0 %collective-permute-done.3 = bf16[256,1792]{1,0:T(8,128)(2,1)} collective-permute-done((bf16[256,1792]{1,0:T(8,128)(2,1)}, bf16[256,1792]{1,0:T(8,128)(2,1)}, u32[]{:S(2)}, u32[]{:S(2)}) %collective-permute-start.3) | collective-permute-done | bytes 917536 | tf_op jit(solution)/shard_map/ppermute | solution.py:18
  206.4 4.4 %fusion.23 = (bf16[1,256,1792]{2,1,0:T(8,128)(2,1)}, bf16[1,256,1792]{2,1,0:T(8,128)(2,1)}) fusion(bf16[1,256,1792]{2,1,0:T(8,128)(2,1)} %param.8, f32[256,1792]{1,0:T(8,128)S(1)} %copy-done, bf16[256,1792]{1,0:T(8,128)(2,1)S(1)} %collective-permute-done.2, pred[]{:T(512)S(6)} %eq.13, bf16[256,1792]{1,0:T(8,128)(2,1)} %collective-permute-done.3, ...), kind=kLoop, calls=%fused_computation.36 | loop fusion | flops 11010048 | bytes 7340034 | tf_op jit(solution)/shard_map/broadcast_in_dim | solution.py:88
  210.7 6.0 %convert_element_type.98 = f32[1792,1024]{1,0:T(8,128)} convert(bf16[1792,1024]{1,0:T(8,128)(2,1)} %reduce-scatter.5.cloned.1.call-done) | non-fusion elementwise | flops 1835008 | bytes 11010048 | tf_op jit(solution)/shard_map/convert_element_type | solution.py:87
  (15 shorter events, 0.2 us)
Async XLA Ops:
  7.2 1.9 copy-start.2
  7.2 47.2 %all-gather.2.cloned.1.call-start = ((), (), s32[]{:S(2)}) async-start(), calls=%async_computation.3 | async-start | bytes 4587520 | tf_op jit(solution)/shard_map/all_gather | solution.py:80
  10.2 89.1 %reduce-scatter.3.cloned.1.call-start = ((), (), s32[]{:S(2)}) async-start(), calls=%async_computation.2 | async-start | bytes 4587520 | tf_op jit(solution)/shard_map/reduce_scatter | solution.py:53
  23.3 187.5 %reduce-scatter.5.cloned.1.call-start = ((), (), s32[]{:S(2)}) async-start(), calls=%async_computation.4 | async-start | bytes 11010048 | tf_op jit(solution)/shard_map/reduce_scatter | solution.py:85
  66.9 32.5 %copy-start.1 = (s32[1,256,1792]{2,1,0:T(8,128)S(1)}, s32[1,256,1792]{2,1,0:T(8,128)}, u32[]{:S(2)}) copy-start(s32[1,256,1792]{2,1,0:T(8,128)} %param.10) | copy-start | bytes 5505028
  109.8 22.6 %collective-permute-start = (bf16[256,1792]{1,0:T(8,128)(2,1)}, bf16[256,1792]{1,0:T(8,128)(2,1)S(1)}, u32[]{:S(2)}, u32[]{:S(2)}) collective-permute-start(bf16[256,1792]{1,0:T(8,128)(2,1)} %convert_element_type.79), channel_id=1, source_target_pairs={{0,8},{8,0},{16,24},{24,16},{32,40},{40,32},{48,56},{56,48},{64,72... | collective-permute-start | bytes 2752520 | tf_op jit(solution)/shard_map/ppermute | solution.py:18
  133.6 23.5 %collective-permute-start.1 = (bf16[256,1792]{1,0:T(8,128)(2,1)}, bf16[256,1792]{1,0:T(8,128)(2,1)}, u32[]{:S(2)}, u32[]{:S(2)}) collective-permute-start(bf16[256,1792]{1,0:T(8,128)(2,1)} %fusion.22), channel_id=1, source_target_pairs={{0,16},{16,0},{8,24},{24,8},{32,48},{48,32},{40,56},{56,40},{64,80... | collective-permute-start | bytes 2752520 | tf_op jit(solution)/shard_map/ppermute | solution.py:18
  160.3 21.2 %collective-permute-start.2 = (bf16[256,1792]{1,0:T(8,128)(2,1)}, bf16[256,1792]{1,0:T(8,128)(2,1)S(1)}, u32[]{:S(2)}, u32[]{:S(2)}) collective-permute-start(bf16[256,1792]{1,0:T(8,128)(2,1)} %get-tuple-element.3), channel_id=1, source_target_pairs={{0,32},{32,0},{8,40},{40,8},{16,48},{48,16},{24,56},{56,24},{64,96... | collective-permute-start | bytes 2752520 | tf_op jit(solution)/shard_map/ppermute | solution.py:18
  181.5 24.8 %copy-start = (f32[256,1792]{1,0:T(8,128)S(1)}, f32[256,1792]{1,0:T(8,128)}, u32[]{:S(2)}) copy-start(f32[256,1792]{1,0:T(8,128)} %get-tuple-element.4) | copy-start | bytes 5505028
  184.3 22.0 %collective-permute-start.3 = (bf16[256,1792]{1,0:T(8,128)(2,1)}, bf16[256,1792]{1,0:T(8,128)(2,1)}, u32[]{:S(2)}, u32[]{:S(2)}) collective-permute-start(bf16[256,1792]{1,0:T(8,128)(2,1)} %fusion.21), channel_id=1, source_target_pairs={{0,64},{64,0},{8,72},{72,8},{16,80},{80,16},{24,88},{88,24},{32,96... | collective-permute-start | bytes 2752520 | tf_op jit(solution)/shard_map/ppermute | solution.py:18
Sparse Core Ops, SparseCore 0:
  10.3 43.9 all-gather.1
  56.8 42.5 reduce-scatter.2
  102.3 93.6 reduce-scatter.4
where the time goes:
time: 224 us; the launch traced here: 223 us
  waiting for transfers between devices  144 us (64%)
  matrix products  28.6 us (13%)
  other arithmetic  22.5 us (10%)
  between operations  13.8 us (6%)
  starting transfers between devices  9.1 us (4%)
  local copies, waits for them, and re-layouts  5.44 us (2%)
    ppermute x4, waiting for transfers between devices, from_partner(): return lax.ppermute(block, axis, route)  80.3 us
    reduce_scatter x1, waiting for transfers between devices, shards(): lax.psum_scatter(lax.dot_general(rows, down_weight, (((1,), (1,)), ((), (...  32.4 us
    all_gather x1, waiting for transfers between devices, shards(): lax.all_gather(dequant, 'wid', axis=0, tiled=True)  31 us
    dot_general x1, matrix products, shards(): lax.dot_general(rows, down_weight, (((1,), (1,)), ((), ())), preferred_el...  13 us
    dot_general x1, matrix products, shards(): lax.dot_general(lax.all_gather(dequant, 'wid', axis=0, tiled=True), rows,...  12.5 us
    ppermute x4, starting transfers between devices, from_partner(): return lax.ppermute(block, axis, route)  8.98 us
    convert_element_type x4, other arithmetic, shards(): mixed.astype(jnp.bfloat16)  8.26 us
    convert_element_type x1, other arithmetic, shards(): grad_down = lax.psum_scatter(replica_term.astype(jnp.bfloat16), 'rep', sc...  5.98 us
  transfers between devices with their start and end apart: 7, of which 6 were waited for; matrix products, arithmetic and copies ran while one was open for 21% of the time, Pallas kernels for 0%

commit v1 on v0

v1 whole, which is shorter than its diff:
```python
import functools
import math

import jax
import jax.numpy as jnp
from jax import lax
from jax.experimental import pallas as pl
from jax.experimental.pallas import tpu as pltpu
from jax.sharding import PartitionSpec as P


BLOCK = 128
TILE = 256
PARTS = ((0, 1792),)
AXES = ("hid", "wid", "rep")
F32 = jnp.float32
BF16 = jnp.bfloat16
ANY_SPEC = pl.BlockSpec(memory_space=pl.ANY)


def send(value, target):
    route = []
    for hid in range(16):
        for wid in range(4):
            for rep in range(2):
                to_hid, to_wid, to_rep = target(hid, wid, rep)
                route.append((hid * 8 + wid * 2 + rep, to_hid * 8 + to_wid * 2 + to_rep))
    return lax.ppermute(value, AXES, route)


def to_mate(hid, wid, rep):
    return hid, wid ^ 1, rep


def to_pair(hid, wid, rep):
    return hid, wid ^ 2, rep


def to_next(hid, wid, rep):
    return hid, wid ^ 2, rep ^ 1


def to_rep(hid, wid, rep):
    return hid, wid, rep ^ 1


def along(axis, step):
    return lambda hid, wid, rep: (hid ^ (step << 2 * ((wid & 1) ^ axis)), wid, rep)


def place(axis):
    hid = lax.axis_index("hid")
    return jnp.where(lax.axis_index("wid") & 1 == axis, hid, hid >> 2) & 3


def dequant_kernel(codes_ref, exponents_ref, out_ref):
    step = pl.program_id(0)
    blocks = out_ref.shape[0] // BLOCK
    for half in range(blocks):
        drop = -exponents_ref[step * blocks + half]
        scale = jnp.where(drop & 1 == 1, 0.5, 1.0) * jnp.where(drop & 2 == 2, 0.25, 1.0)
        scale = scale * jnp.where(drop & 4 == 4, 2.0 ** -4, 1.0) * jnp.where(drop & 8 == 8, 2.0 ** -8, 1.0)
        span = pl.ds(half * BLOCK, BLOCK)
        out_ref[span, :] = (codes_ref[:, span].astype(F32).T * scale).astype(BF16)


def dequant_t(codes, exponents_t):
    tokens, hidden = codes.shape
    tile = hidden // 2
    return pl.pallas_call(
        dequant_kernel,
        out_shape=jax.ShapeDtypeStruct((hidden, tokens), BF16),
        grid=(hidden // tile,),
        in_specs=[pl.BlockSpec((tokens, tile), lambda i: (0, i)), pl.BlockSpec(exponents_t.shape, lambda i: (0, 0, 0))],
        out_specs=pl.BlockSpec((tile, tokens), lambda i: (i, 0)),
        compiler_params=pltpu.CompilerParams(vmem_limit_bytes=12 << 20),
        name="dequant",
    )(codes, exponents_t)


def grad_quant_kernel(rows_ref, w_ref, far_away, far_keep, near_away, near_keep, total_ref):
    tokens = far_away.shape[0]
    wid = lax.axis_index("wid")
    total_ref[...] = lax.dot_general(
        rows_ref[...], w_ref[...], (((1,), (1,)), ((), ())), preferred_element_type=F32).astype(BF16)
    for flip, out in ((3, far_away), (2, far_keep), (1, near_away), (0, near_keep)):
        out[...] = total_ref[pl.ds(pl.multiple_of((wid ^ flip) * tokens, tokens), tokens), :]


def grad_quant(rows, weight, first, count):
    total, width = rows.shape
    tokens = total // 4
    return pl.pallas_call(
        grad_quant_kernel,
        out_shape=[jax.ShapeDtypeStruct((tokens, count), BF16)] * 4,
        grid=(count // TILE,),
        in_specs=[pl.BlockSpec((total, width), lambda i: (0, 0)),
                  pl.BlockSpec((TILE, width), lambda i: (i + first // TILE, 0))],
        out_specs=[pl.BlockSpec((tokens, TILE), lambda i: (0, i))] * 4,
        scratch_shapes=[pltpu.VMEM((total, TILE), BF16)],
        name="grad_quant",
    )(rows, weight)


SMALL = pltpu.CompilerParams(vmem_limit_bytes=12 << 20)
VMEM_SPEC = pl.BlockSpec(memory_space=pltpu.VMEM)


def rotate_kernel(*refs, scale, parts):
    codes_ref = refs[3 * len(parts)]
    outs = refs[3 * len(parts) + 1:]
    rows = outs[0].shape[0]
    mine = place(0)
    row = lax.broadcasted_iota(jnp.int32, (TILE, TILE), 0)
    col = lax.broadcasted_iota(jnp.int32, (TILE, TILE), 1)
    bits = row & col & (BLOCK - 1)
    for shift in (4, 2, 1):
        bits = bits ^ (bits >> shift)
    sign = (1 - 2 * (bits & 1)).astype(F32)
    table = jnp.where((row ^ col) < BLOCK, sign, 0.0).astype(BF16)
    for part, (start, count) in enumerate(parts):
        keep_ref, away_ref, far_ref = refs[3 * part:3 * part + 3]
        for first in range(0, count, TILE):
            here = pl.ds(first, TILE)
            cols = pl.ds(start + first, TILE)
            total = keep_ref[:, here].astype(F32) + away_ref[:, here].astype(F32) + far_ref[:, here].astype(F32)
            codes = codes_ref[:, cols]
            masked = jnp.where((codes > -128) & (codes < 127), total, 0.0).astype(BF16)
            mixed = (jnp.dot(masked, table, preferred_element_type=F32) * scale).astype(BF16)
            for quarter in range(4):
                piece = mixed[quarter * rows:(quarter + 1) * rows]
                for step, out in enumerate(outs):
                    @pl.when(mine ^ step == quarter)
                    def _():
                        out[:, cols] = piece


def rotate(sums, codes, scale):
    tokens, hidden = codes.shape
    return pl.pallas_call(
        functools.partial(rotate_kernel, scale=scale, parts=PARTS),
        out_shape=[pltpu.VMEM((tokens // 4, hidden), BF16)] * 4,
        in_specs=[VMEM_SPEC] * (3 * len(PARTS) + 1),
        out_specs=[VMEM_SPEC] * 4,
        compiler_params=SMALL,
        name="rotate",
    )(*[value for group in sums for value in group], codes)


def parity(value):
    return (1 - 2 * ((value ^ (value >> 1)) & 1)).astype(F32)


def mix_kernel(*refs, axis):
    mine = place(axis)
    signs = [parity(mine & step) for step in range(4)]
    whole = parity(mine)
    hidden = refs[0].shape[1]
    for first in range(0, hidden, TILE):
        cols = pl.ds(first, TILE)
        p0, p1, p2, p3 = [refs[step][:, cols].astype(F32) * signs[step] for step in range(4)]
        even, odd = (p0 + p1, p2 + p3), (p0 - p1, p2 - p3)
        outs = (even[0] + even[1], odd[0] + odd[1], even[0] - even[1], odd[0] - odd[1])
        for step in range(4):
            refs[4 + step][:, cols] = (outs[step] * (whole * signs[step])).astype(BF16)


def relabel_kernel(*refs):
    turn = place(0) ^ place(1)
    for step in range(4):
        for other in range(4):
            @pl.when(turn == step ^ other)
            def _():
                refs[4 + step][...] = refs[other][...]


def four(kernel, pieces):
    return pl.pallas_call(
        kernel,
        out_shape=[pltpu.VMEM(pieces[0].shape, BF16)] * 4,
        in_specs=[VMEM_SPEC] * 4,
        out_specs=[VMEM_SPEC] * 4,
        compiler_params=SMALL,
    )(*pieces)


def finish_kernel(p0, p1, p2, p3, gate_ref, up_ref, gate_out, up_out):
    mine = place(1)
    rows = p0.shape[0]
    for step, piece in enumerate((p0, p1, p2, p3)):
        span = pl.ds(pl.multiple_of((mine ^ step) * rows, rows), rows)
        for first in range(0, piece.shape[1], TILE):
            cols = pl.ds(first, TILE)
            hidden = piece[:, cols].astype(F32)
            gate = gate_ref[span, cols].astype(F32)
            up = up_ref[span, cols].astype(F32)
            sig = jax.nn.sigmoid(gate)
            gate_out[span, cols] = (hidden * up * sig * (1.0 + gate * (1.0 - sig))).astype(BF16)
            up_out[span, cols] = (hidden * gate * sig).astype(BF16)


def finish(pieces, gate, up):
    return pl.pallas_call(
        finish_kernel,
        out_shape=[jax.ShapeDtypeStruct(gate.shape, BF16)] * 2,
        in_specs=[VMEM_SPEC] * 6,
        out_specs=[VMEM_SPEC] * 2,
        compiler_params=SMALL,
        name="finish",
    )(*pieces, gate, up)


def down_kernel(*refs, flips, remote, summed):
    count = len(flips)
    pieces, sources = refs[:count], refs[count:-4 - summed]
    out_ref, lhs_ref, rhs_ref, sem = refs[-4:]
    tokens = pieces[0].shape[1]
    width = rhs_ref.shape[1]
    step = pl.program_id(0)
    cols = pl.ds(pl.multiple_of(step * TILE, TILE), TILE)

    def store(total):
        if summed:
            total = total + refs[-5][...].astype(F32)
        out_ref[...] = total.astype(out_ref.dtype)

    @pl.when(step == 0)
    def _():
        hid = lax.axis_index("hid")
        wid = lax.axis_index("wid")
        first_col = pl.multiple_of(lax.axis_index("rep") * width, width)
        quarter = ((hid >> 2) & 1) * 2 + (hid & 1)
        left = [pltpu.make_async_copy(piece, lhs_ref.at[:, pl.ds(i * tokens, tokens)], sem.at[i])
                for i, piece in enumerate(pieces)]
        right = []
        for i, flip in enumerate(flips):
            left[i].start()
            target = rhs_ref.at[pl.ds(i * tokens, tokens)]
            if not remote:
                span = pl.ds(pl.multiple_of((wid ^ flip) * tokens, tokens), tokens)
                right.append(pltpu.make_async_copy(sources[0].at[span, pl.ds(first_col, width)], target, sem.at[count + i]))
                right[i].start()
                continue
            g0, g1, g23 = sources
            where = quarter ^ wid ^ flip
            index = jnp.where(wid & 1 == 0, where, (where >> 1) | ((where & 1) << 1))
            for number, source in enumerate((g0, g1, g23.at[0], g23.at[1])):
                @pl.when(index == number)
                def _():
                    pltpu.make_async_copy(source, target, sem.at[count + i]).start()
            right.append(pltpu.make_async_copy(g0, target, sem.at[count + i]))
        total = None
        for i in range(count):
            left[i].wait()
            right[i].wait()
            part = jnp.dot(lhs_ref[:, i * tokens:(i + 1) * tokens], rhs_ref[i * tokens:(i + 1) * tokens, :TILE],
                           preferred_element_type=F32)
            total = part if total is None else total + part
        store(total)

    @pl.when(step > 0)
    def _():
        store(jnp.dot(lhs_ref[...], rhs_ref[:, cols], preferred_element_type=F32))


def down(pieces, flips, sources, width, acc=None, dtype=BF16):
    hidden, tokens = pieces[0].shape
    count = len(pieces)
    spec = pl.BlockSpec((hidden, TILE), lambda i: (0, i))
    return pl.pallas_call(
        functools.partial(down_kernel, flips=flips, remote=len(sources) > 1, summed=acc is not None),
        out_shape=jax.ShapeDtypeStruct((hidden, width), dtype),
        grid=(width // TILE,),
        in_specs=[ANY_SPEC] * (count + len(sources)) + [spec] * (acc is not None),
        out_specs=spec,
        scratch_shapes=[pltpu.VMEM((hidden, count * tokens), BF16), pltpu.VMEM((count * tokens, width), BF16),
                        pltpu.SemaphoreType.DMA((2 * count,))],
        name="down",
    )(*pieces, *sources, *(() if acc is None else (acc,)))


def shards(grad_out, down_weight, saved_gate, saved_up, saved_codes, exponents):
    rows = grad_out[0]
    codes = saved_codes[0]
    tokens = codes.shape[0]
    half = rows.shape[1] // 2
    hid = lax.axis_index("hid")
    wid = lax.axis_index("wid")
    rep = lax.axis_index("rep")
    core = wid & 1
    scale = 1.0 / math.sqrt(BLOCK * 16)

    quarter = ((hid >> 2) & 1) * 2 + (hid & 1)
    g0 = lax.dynamic_slice(rows, (quarter * tokens, (1 - rep) * half), (tokens, half))
    g0 = send(g0, to_rep)
    g1 = send(g0, lambda h, w, r: (h ^ (3 if w & 1 == 0 else 12), w, r))
    g23 = send(jnp.stack([g0, g1]), lambda h, w, r: (h ^ (12 if w & 1 == 0 else 3), w, r))
    others = (g0, g1, g23)

    own = dequant_t(codes, jnp.transpose(exponents, (2, 0, 1)))
    own_mate = send(own, to_mate)
    next_ = send(own, to_next)
    next_mate = send(next_, to_mate)

    sums = []
    for first, count in PARTS:
        far_away, far_keep, near_away, near_keep = grad_quant(rows, down_weight, first, count)
        far_away = send(far_away, to_mate)
        near_away = send(near_away, to_mate)
        far = (far_keep.astype(F32) + far_away.astype(F32)).astype(BF16)
        far = send(far, to_pair)
        sums.append((near_keep, near_away, far))

    pair = send(own, to_pair)
    pair_mate = send(pair, to_mate)
    cross = jnp.where(core == 0, pair, next_)
    cross = send(cross, lambda h, w, r: (h, w ^ 2, r ^ 1 if w & 1 == 0 else r))
    cross_mate = send(cross, to_mate)

    product = down((own, own_mate), (0, 1), (rows,), half)
    product = down((next_, next_mate), (2, 3), others, half, product)
    product = down((pair, pair_mate), (2, 3), (rows,), half, product)

    def spread(pieces, axis):
        moved = list(pieces)
        for step in (2, 1, 3):
            moved[step] = send(pieces[step], along(axis, step))
        return moved

    pieces = rotate(sums, codes, scale)
    pieces = spread(pieces, 0)
    pieces = four(functools.partial(mix_kernel, axis=0), pieces)
    pieces = spread(pieces, 0)
    pieces = four(relabel_kernel, pieces)
    pieces = spread(pieces, 1)
    pieces = four(functools.partial(mix_kernel, axis=1), pieces)
    pieces = spread(pieces, 1)
    grad_gate, grad_up = finish(pieces, saved_gate[0], saved_up[0])

    grad_down = down((cross, cross_mate), (0, 1), others, half, product, F32)
    return grad_gate[None], grad_up[None], grad_down


def solution(mesh):
    in_specs = (
        P("rep", None, "wid"),
        P("hid", "wid"),
        P("rep", "wid", "hid"),
        P("rep", "wid", "hid"),
        P("rep", "wid", "hid"),
        P("rep", "wid", "hid"),
    )
    out_specs = (P("rep", "wid", "hid"), P("rep", "wid", "hid"), P("hid", ("wid", "rep")))


    return jax.shard_map(shards, mesh=mesh, in_specs=in_specs, out_specs=out_specs, check_vma=False)
```

time: 224 us -> 167 us (0.75)
  waiting for transfers between devices: 144 us -> 72.8 us
  Pallas kernels: 0 us -> 50.1 us
  matrix products: 28.6 us -> 0 us
  starting transfers between devices: 9.1 us -> 34.8 us
  other arithmetic: 22.5 us -> 3.72 us
  between operations: 13.8 us -> 0.89 us
  local copies, waits for them, and re-layouts: 5.44 us -> 3.09 us
    pallas_call x0 -> x11, Pallas kernels: none -> 50.1 us  [the longest x4 29.4 us: down(): pl.pallas_call(functools.partial(down_kernel, flips=flips, remote=len(sou...]
    reduce_scatter x2 -> x0, waiting for transfers between devices: 32.4 us -> none  [the longest x1 32.4 us: shards(): lax.psum_scatter(lax.dot_general(rows, down_weight, (((1,), (1,)), ((), (...]
    all_gather x1 -> x0, waiting for transfers between devices: 31 us -> none  [shards(): lax.all_gather(dequant, 'wid', axis=0, tiled=True)]
    dot_general x3 -> x0, matrix products: 28.6 us -> none  [the longest x1 13 us: shards(): lax.dot_general(rows, down_weight, (((1,), (1,)), ((), ())), preferred_el...]
    ppermute x4 -> x25, starting transfers between devices: 8.98 us -> 34.8 us  [send(): return lax.ppermute(value, AXES, route)]
    convert_element_type x6 -> x1, other arithmetic: 15.3 us -> 2.35 us  [shards(): far = (far_keep.astype(F32) + far_away.astype(F32)).astype(BF16)]
    ppermute x4 -> x25, waiting for transfers between devices: 80.3 us -> 72.8 us  [send(): return lax.ppermute(value, AXES, route)]
    broadcast_in_dim x1 -> x0, other arithmetic: 4.38 us -> none  [shards(): return (grad_gate[None], grad_up[None], grad_down)]
  transfers between devices with their start and end apart: 7 -> 25, of which waited for: 6 -> 12; matrix products, arithmetic and copies ran while one was open for 21% -> 3% of each run, Pallas kernels for 0% -> 21%
where the time goes in v1:
time: 167 us; the launch traced here: 165 us
  waiting for transfers between devices  72.8 us (44%)
  Pallas kernels  50.1 us (30%)
  starting transfers between devices  34.8 us (21%)
  other arithmetic  3.72 us (2%)
  local copies, waits for them, and re-layouts  3.09 us (2%)
    ppermute x25, waiting for transfers between devices, send(): return lax.ppermute(value, AXES, route)  72.8 us
    ppermute x25, starting transfers between devices, send(): return lax.ppermute(value, AXES, route)  34.8 us
    pallas_call x4, Pallas kernels, down(): pl.pallas_call(functools.partial(down_kernel, flips=flips, remote=len(sou...  29.4 us
    pallas_call x1, Pallas kernels, grad_quant(): pl.pallas_call(grad_quant_kernel, out_shape=[jax.ShapeDtypeStruct((tokens...  13 us
    pallas_call x1, Pallas kernels, rotate(): pl.pallas_call(functools.partial(rotate_kernel, scale=scale, parts=PARTS)...  3.44 us
  transfers between devices with their start and end apart: 25, of which 12 were waited for; matrix products, arithmetic and copies ran while one was open for 3% of the time, Pallas kernels for 21%

profile of v1, /device:TPU:0, one launch (start us, length us, event | category | flops | bytes accessed | tf_op | source)
XLA Modules:
  0.0 165.5 jit_solution(14449222220447350956)
XLA Ops:
  0.7 13.0 %grad_quant.1 = (bf16[256,1792]{1,0:T(8,128)(2,1)}, bf16[256,1792]{1,0:T(8,128)(2,1)}, bf16[256,1792]{1,0:T(8,128)(2,1)}, bf16[256,1792]{1,0:T(8,128)(2,1)}) custom-call(bf16[1024,2048]{1,0:T(8,128)(2,1)} %bitcast.16, bf16[1792,2048]{1,0:T(8,128)(2,1)} %w_ref.1), custom_call_target="tpu_custom_call" | custom-call | tf_op jit(solution)/shard_map/grad_quant/pallas_call | solution.py:93
  14.5 4.2 %collective-permute-start.16 = (bf16[1792,256]{1,0:T(8,128)(2,1)S(1)}, bf16[1792,256]{1,0:T(8,128)(2,1)}, u32[]{:S(2)}, u32[]{:S(2)}) collective-permute-start(bf16[1792,256]{1,0:T(8,128)(2,1)S(1)} %dequant.1.refs_0_), channel_id=1, source_target_pairs={{0,5},{1,4},{2,7},{3,6},{4,1},{5,0},{6,3},{7,2},{8,13},{9,12},{10,... | collective-permute-start | bytes 2752520 | tf_op jit(solution)/shard_map/ppermute | solution.py:28
  18.9 2.3 %add_convert_fusion = bf16[256,1792]{1,0:T(8,128)(2,1)} fusion(bf16[256,1792]{1,0:T(8,128)(2,1)S(1)} %collective-permute-done.1, bf16[256,1792]{1,0:T(8,128)(2,1)} %get-tuple-element.27), kind=kLoop, calls=%fused_computation | loop fusion | flops 1835008 | bytes 2752512 | tf_op jit(solution)/shard_map/convert_element_type | solution.py:310
  26.2 13.6 %collective-permute-done.16.refs_0_ = bf16[1792,256]{1,0:T(8,128)(2,1)} collective-permute-done((bf16[1792,256]{1,0:T(8,128)(2,1)S(1)}, bf16[1792,256]{1,0:T(8,128)(2,1)}, u32[]{:S(2)}, u32[]{:S(2)}) %collective-permute-start.16) | collective-permute-done | bytes 917536 | tf_op jit(solution)/shard_map/ppermute | solution.py:28
  39.8 2.2 %collective-permute-done.15.refs_0_ = bf16[1792,256]{1,0:T(8,128)(2,1)} collective-permute-done((bf16[1792,256]{1,0:T(8,128)(2,1)S(1)}, bf16[1792,256]{1,0:T(8,128)(2,1)}, u32[]{:S(2)}, u32[]{:S(2)}) %collective-permute-start.15) | collective-permute-done | bytes 917536 | tf_op jit(solution)/shard_map/ppermute | solution.py:28
  44.1 28.2 %collective-permute-done.19.refs_2_ = bf16[256,1024]{1,0:T(8,128)(2,1)S(1)} collective-permute-done((bf16[256,1024]{1,0:T(8,128)(2,1)}, bf16[256,1024]{1,0:T(8,128)(2,1)S(1)}, u32[]{:S(2)}, u32[]{:S(2)}) %collective-permute-start.19) | collective-permute-done | bytes 524320 | tf_op jit(solution)/shard_map/ppermute | solution.py:28
  72.4 3.0 %collective-permute-start.20 = (bf16[256,1024]{1,0:T(8,128)(2,1)S(1)}, bf16[256,1024]{1,0:T(8,128)(2,1)S(1)}, u32[]{:S(2)}, u32[]{:S(2)}) collective-permute-start(bf16[256,1024]{1,0:T(8,128)(2,1)S(1)} %collective-permute-done.19.refs_2_), channel_id=1, source_target_pairs={{0,24},{1,25},{2,98},{3,99},{4,28},{5,29},{6,102},{7,103},{8,16},{... | collective-permute-start | bytes 1572872 | tf_op jit(solution)/shard_map/ppermute | solution.py:28
  76.6 3.4 %rotate.1 = (bf16[64,1792]{1,0:T(8,128)(2,1)S(1)}, bf16[64,1792]{1,0:T(8,128)(2,1)S(1)}, bf16[64,1792]{1,0:T(8,128)(2,1)S(1)}, bf16[64,1792]{1,0:T(8,128)(2,1)S(1)}) custom-call(bf16[256,1792]{1,0:T(8,128)(2,1)S(1)} %copy-done.4, bf16[256,1792]{1,0:T(8,128)(2,1)} %collective-permute-done.refs_1_, bf16[256,1792]{1,0:T(8,128)(2,1)} %collective-permute-done.2.refs_2_, ...), custom_call_target="tpu_custom_call" | custom-call | tf_op jit(solution)/shard_map/rotate/pallas_call | solution.py:140
  81.7 3.0 %collective-permute-start.5 = (bf16[64,1792]{1,0:T(8,128)(2,1)S(1)}, bf16[64,1792]{1,0:T(8,128)(2,1)S(1)}, u32[]{:S(2)}, u32[]{:S(2)}) collective-permute-start(bf16[64,1792]{1,0:T(8,128)(2,1)S(1)} %get-tuple-element.32), channel_id=1, source_target_pairs={{0,24},{1,25},{2,98},{3,99},{4,28},{5,29},{6,102},{7,103},{8,16},{... | collective-permute-start | bytes 688136 | tf_op jit(solution)/shard_map/ppermute | solution.py:28
  86.1 2.2 %collective-permute-done.4.refs_2_ = bf16[64,1792]{1,0:T(8,128)(2,1)S(1)} collective-permute-done((bf16[64,1792]{1,0:T(8,128)(2,1)S(1)}, bf16[64,1792]{1,0:T(8,128)(2,1)S(1)}, u32[]{:S(2)}, u32[]{:S(2)}) %collective-permute-start.4) | collective-permute-done | bytes 229408 | tf_op jit(solution)/shard_map/ppermute | solution.py:28
  88.3 2.4 %collective-permute-done.5.refs_3_ = bf16[64,1792]{1,0:T(8,128)(2,1)S(1)} collective-permute-done((bf16[64,1792]{1,0:T(8,128)(2,1)S(1)}, bf16[64,1792]{1,0:T(8,128)(2,1)S(1)}, u32[]{:S(2)}, u32[]{:S(2)}) %collective-permute-start.5) | collective-permute-done | bytes 229408 | tf_op jit(solution)/shard_map/ppermute | solution.py:28
  91.1 4.5 %collective-permute-start.7 = (bf16[64,1792]{1,0:T(8,128)(2,1)S(1)}, bf16[64,1792]{1,0:T(8,128)(2,1)S(1)}, u32[]{:S(2)}, u32[]{:S(2)}) collective-permute-start(bf16[64,1792]{1,0:T(8,128)(2,1)S(1)} %get-tuple-element.35), channel_id=1, source_target_pairs={{0,16},{1,17},{2,66},{3,67},{4,20},{5,21},{6,70},{7,71},{8,24},{9,... | collective-permute-start | bytes 688136 | tf_op jit(solution)/shard_map/ppermute | solution.py:28
  97.1 5.0 %collective-permute-done.7.refs_2_ = bf16[64,1792]{1,0:T(8,128)(2,1)S(1)} collective-permute-done((bf16[64,1792]{1,0:T(8,128)(2,1)S(1)}, bf16[64,1792]{1,0:T(8,128)(2,1)S(1)}, u32[]{:S(2)}, u32[]{:S(2)}) %collective-permute-start.7) | collective-permute-done | bytes 229408 | tf_op jit(solution)/shard_map/ppermute | solution.py:28
  102.1 2.4 %collective-permute-done.8.refs_3_ = bf16[64,1792]{1,0:T(8,128)(2,1)S(1)} collective-permute-done((bf16[64,1792]{1,0:T(8,128)(2,1)S(1)}, bf16[64,1792]{1,0:T(8,128)(2,1)S(1)}, u32[]{:S(2)}, u32[]{:S(2)}) %collective-permute-start.8) | collective-permute-done | bytes 229408 | tf_op jit(solution)/shard_map/ppermute | solution.py:28
  104.6 2.2 %collective-permute-start.9 = (bf16[64,1792]{1,0:T(8,128)(2,1)S(1)}, bf16[64,1792]{1,0:T(8,128)(2,1)S(1)}, u32[]{:S(2)}, u32[]{:S(2)}) collective-permute-start(bf16[64,1792]{1,0:T(8,128)(2,1)S(1)} %get-tuple-element.38), channel_id=1, source_target_pairs={{0,32},{1,33},{2,10},{3,11},{4,36},{5,37},{6,14},{7,15},{8,40},{9,... | collective-permute-start | bytes 688136 | tf_op jit(solution)/shard_map/ppermute | solution.py:28
  106.9 3.2 %collective-permute-start.21 = (bf16[2,256,1024]{2,1,0:T(8,128)(2,1)S(1)}, bf16[2,256,1024]{2,1,0:T(8,128)(2,1)S(1)}, u32[]{:S(2)}, u32[]{:S(2)}) collective-permute-start(bf16[2,256,1024]{2,1,0:T(8,128)(2,1)S(1)} %pad_maximum_fusion), channel_id=1, source_target_pairs={{0,96},{1,97},{2,26},{3,27},{4,100},{5,101},{6,30},{7,31},{8,104},... | collective-permute-start | bytes 3145736 | tf_op jit(solution)/shard_map/ppermute | solution.py:28
  110.8 3.1 %collective-permute-start.11 = (bf16[64,1792]{1,0:T(8,128)(2,1)S(1)}, bf16[64,1792]{1,0:T(8,128)(2,1)S(1)}, u32[]{:S(2)}, u32[]{:S(2)}) collective-permute-start(bf16[64,1792]{1,0:T(8,128)(2,1)S(1)} %get-tuple-element.40), channel_id=1, source_target_pairs={{0,96},{1,97},{2,26},{3,27},{4,100},{5,101},{6,30},{7,31},{8,104},... | collective-permute-start | bytes 688136 | tf_op jit(solution)/shard_map/ppermute | solution.py:28
  113.9 4.3 %collective-permute-done.10.refs_2_ = bf16[64,1792]{1,0:T(8,128)(2,1)S(1)} collective-permute-done((bf16[64,1792]{1,0:T(8,128)(2,1)S(1)}, bf16[64,1792]{1,0:T(8,128)(2,1)S(1)}, u32[]{:S(2)}, u32[]{:S(2)}) %collective-permute-start.10) | collective-permute-done | bytes 229408 | tf_op jit(solution)/shard_map/ppermute | solution.py:28
  118.3 9.6 %collective-permute-done.11.refs_3_ = bf16[64,1792]{1,0:T(8,128)(2,1)S(1)} collective-permute-done((bf16[64,1792]{1,0:T(8,128)(2,1)S(1)}, bf16[64,1792]{1,0:T(8,128)(2,1)S(1)}, u32[]{:S(2)}, u32[]{:S(2)}) %collective-permute-start.11) | collective-permute-done | bytes 229408 | tf_op jit(solution)/shard_map/ppermute | solution.py:28
  128.8 4.6 %collective-permute-start.13 = (bf16[64,1792]{1,0:T(8,128)(2,1)S(1)}, bf16[64,1792]{1,0:T(8,128)(2,1)S(1)}, u32[]{:S(2)}, u32[]{:S(2)}) collective-permute-start(bf16[64,1792]{1,0:T(8,128)(2,1)S(1)} %get-tuple-element.43), channel_id=1, source_target_pairs={{0,64},{1,65},{2,18},{3,19},{4,68},{5,69},{6,22},{7,23},{8,72},{9,... | collective-permute-start | bytes 688136 | tf_op jit(solution)/shard_map/ppermute | solution.py:28
  133.8 5.6 %down.4.refs_5_ = bf16[1792,1024]{1,0:T(8,128)(2,1)} custom-call(bf16[1792,256]{1,0:T(8,128)(2,1)} %copy-done.1, bf16[1792,256]{1,0:T(8,128)(2,1)} %copy-done.9, bf16[1024,2048]{1,0:T(8,128)(2,1)} %bitcast.17), custom_call_target="tpu_custom_call" | custom-call | tf_op jit(solution)/shard_map/down/pallas_call | solution.py:270
  139.4 7.6 %down.5.refs_3_ = bf16[1792,1024]{1,0:T(8,128)(2,1)} custom-call(bf16[1792,256]{1,0:T(8,128)(2,1)} %collective-permute-done.16.refs_0_, bf16[1792,256]{1,0:T(8,128)(2,1)} %copy-done.10, bf16[256,1024]{1,0:T(8,128)(2,1)} %copy-done.6, bf16[256,1024]{1,0:T(8,128)(2,1)} %copy-done.7, bf16[2,256,1024]{2,1,0:T(8,128)(2,1)} %copy-done.8, ...), custom_call_target="tpu_custom_call" | custom-call | tf_op jit(solution)/shard_map/down/pallas_call | solution.py:270
  147.1 7.6 %down.6.refs_5_ = bf16[1792,1024]{1,0:T(8,128)(2,1)} custom-call(bf16[1792,256]{1,0:T(8,128)(2,1)} %collective-permute-done.15.refs_0_, bf16[1792,256]{1,0:T(8,128)(2,1)} %collective-permute-done.22.refs_1_, bf16[1024,2048]{1,0:T(8,128)(2,1)} %bitcast.18, bf16[1792,1024]{1,0:T(8,128)(2,1)} %down.5.refs_3_), custom_call_target="tpu_custom_call" | custom-call | tf_op jit(solution)/shard_map/down/pallas_call | solution.py:270
  154.7 8.6 %down.7 = f32[1792,1024]{1,0:T(8,128)} custom-call(bf16[1792,256]{1,0:T(8,128)(2,1)} %collective-permute-done.17.refs_0_, bf16[1792,256]{1,0:T(8,128)(2,1)} %collective-permute-done.18.refs_1_, bf16[256,1024]{1,0:T(8,128)(2,1)} %copy-done.6, bf16[256,1024]{1,0:T(8,128)(2,1)} %copy-done.7, bf16[2,256,1024]{2,1,0:T(8,128)(2,1)} %copy-done.8, ...), custom_call_target="tpu_custom_call" | custom-call | tf_op jit(solution)/shard_map/down/pallas_call | solution.py:270
  (63 shorter events, 18.5 us)
Async XLA Ops:
  14.5 25.3 %collective-permute-start.16 = (bf16[1792,256]{1,0:T(8,128)(2,1)S(1)}, bf16[1792,256]{1,0:T(8,128)(2,1)}, u32[]{:S(2)}, u32[]{:S(2)}) collective-permute-start(bf16[1792,256]{1,0:T(8,128)(2,1)S(1)} %dequant.1.refs_0_), channel_id=1, source_target_pairs={{0,5},{1,4},{2,7},{3,6},{4,1},{5,0},{6,3},{7,2},{8,13},{9,12},{10,... | collective-permute-start | bytes 2752520 | tf_op jit(solution)/shard_map/ppermute | solution.py:28
  18.7 23.3 %collective-permute-start.15 = (bf16[1792,256]{1,0:T(8,128)(2,1)S(1)}, bf16[1792,256]{1,0:T(8,128)(2,1)}, u32[]{:S(2)}, u32[]{:S(2)}) collective-permute-start(bf16[1792,256]{1,0:T(8,128)(2,1)S(1)} %dequant.1.refs_0_), channel_id=1, source_target_pairs={{0,4},{1,5},{2,6},{3,7},{4,0},{5,1},{6,2},{7,3},{8,12},{9,13},{10,... | collective-permute-start | bytes 2752520 | tf_op jit(solution)/shard_map/ppermute | solution.py:28
  18.7 56.7 %collective-permute-start = (bf16[256,1792]{1,0:T(8,128)(2,1)}, bf16[256,1792]{1,0:T(8,128)(2,1)}, u32[]{:S(2)}, u32[]{:S(2)}) collective-permute-start(bf16[256,1792]{1,0:T(8,128)(2,1)} %get-tuple-element.26), channel_id=1, source_target_pairs={{0,2},{1,3},{2,0},{3,1},{4,6},{5,7},{6,4},{7,5},{8,10},{9,11},{10,... | collective-permute-start | bytes 2752520 | tf_op jit(solution)/shard_map/ppermute | solution.py:28
  21.3 54.1 %collective-permute-start.2 = (bf16[256,1792]{1,0:T(8,128)(2,1)}, bf16[256,1792]{1,0:T(8,128)(2,1)}, u32[]{:S(2)}, u32[]{:S(2)}) collective-permute-start(bf16[256,1792]{1,0:T(8,128)(2,1)} %add_convert_fusion), channel_id=1, source_target_pairs={{0,4},{1,5},{2,6},{3,7},{4,0},{5,1},{6,2},{7,3},{8,12},{9,13},{10,... | collective-permute-start | bytes 2752520 | tf_op jit(solution)/shard_map/ppermute | solution.py:28
  24.9 47.4 %collective-permute-start.19 = (bf16[256,1024]{1,0:T(8,128)(2,1)}, bf16[256,1024]{1,0:T(8,128)(2,1)S(1)}, u32[]{:S(2)}, u32[]{:S(2)}) collective-permute-start(bf16[256,1024]{1,0:T(8,128)(2,1)} %dynamic-slice_bitcast_fusion), channel_id=1, source_target_pairs={{0,1},{1,0},{2,3},{3,2},{4,5},{5,4},{6,7},{7,6},{8,9},{9,8},{10,11... | collective-permute-start | bytes 1572872 | tf_op jit(solution)/shard_map/ppermute | solution.py:28
  43.3 67.3 %collective-permute-start.17 = (bf16[1792,256]{1,0:T(8,128)(2,1)S(1)}, bf16[1792,256]{1,0:T(8,128)(2,1)}, u32[]{:S(2)}, u32[]{:S(2)}) collective-permute-start(bf16[1792,256]{1,0:T(8,128)(2,1)S(1)} %broadcast_select_fusion), channel_id=1, source_target_pairs={{0,5},{1,4},{2,6},{3,7},{4,1},{5,0},{6,2},{7,3},{8,13},{9,12},{10,... | collective-permute-start | bytes 2752520 | tf_op jit(solution)/shard_map/ppermute | solution.py:28
  72.4 34.4 %collective-permute-start.20 = (bf16[256,1024]{1,0:T(8,128)(2,1)S(1)}, bf16[256,1024]{1,0:T(8,128)(2,1)S(1)}, u32[]{:S(2)}, u32[]{:S(2)}) collective-permute-start(bf16[256,1024]{1,0:T(8,128)(2,1)S(1)} %collective-permute-done.19.refs_2_), channel_id=1, source_target_pairs={{0,24},{1,25},{2,98},{3,99},{4,28},{5,29},{6,102},{7,103},{8,16},{... | collective-permute-start | bytes 1572872 | tf_op jit(solution)/shard_map/ppermute | solution.py:28
  80.0 6.1 %collective-permute-start.3 = (bf16[64,1792]{1,0:T(8,128)(2,1)S(1)}, bf16[64,1792]{1,0:T(8,128)(2,1)S(1)}, u32[]{:S(2)}, u32[]{:S(2)}) collective-permute-start(bf16[64,1792]{1,0:T(8,128)(2,1)S(1)} %get-tuple-element.30), channel_id=1, source_target_pairs={{0,8},{1,9},{2,34},{3,35},{4,12},{5,13},{6,38},{7,39},{8,0},{9,1},... | collective-permute-start | bytes 688136 | tf_op jit(solution)/shard_map/ppermute | solution.py:28
  80.2 8.1 %collective-permute-start.4 = (bf16[64,1792]{1,0:T(8,128)(2,1)S(1)}, bf16[64,1792]{1,0:T(8,128)(2,1)S(1)}, u32[]{:S(2)}, u32[]{:S(2)}) collective-permute-start(bf16[64,1792]{1,0:T(8,128)(2,1)S(1)} %get-tuple-element.31), channel_id=1, source_target_pairs={{0,16},{1,17},{2,66},{3,67},{4,20},{5,21},{6,70},{7,71},{8,24},{9,... | collective-permute-start | bytes 688136 | tf_op jit(solution)/shard_map/ppermute | solution.py:28
  81.7 8.9 %collective-permute-start.5 = (bf16[64,1792]{1,0:T(8,128)(2,1)S(1)}, bf16[64,1792]{1,0:T(8,128)(2,1)S(1)}, u32[]{:S(2)}, u32[]{:S(2)}) collective-permute-start(bf16[64,1792]{1,0:T(8,128)(2,1)S(1)} %get-tuple-element.32), channel_id=1, source_target_pairs={{0,24},{1,25},{2,98},{3,99},{4,28},{5,29},{6,102},{7,103},{8,16},{... | collective-permute-start | bytes 688136 | tf_op jit(solution)/shard_map/ppermute | solution.py:28
  91.0 6.1 %collective-permute-start.6 = (bf16[64,1792]{1,0:T(8,128)(2,1)S(1)}, bf16[64,1792]{1,0:T(8,128)(2,1)S(1)}, u32[]{:S(2)}, u32[]{:S(2)}) collective-permute-start(bf16[64,1792]{1,0:T(8,128)(2,1)S(1)} %get-tuple-element.34), channel_id=1, source_target_pairs={{0,8},{1,9},{2,34},{3,35},{4,12},{5,13},{6,38},{7,39},{8,0},{9,1},... | collective-permute-start | bytes 688136 | tf_op jit(solution)/shard_map/ppermute | solution.py:28
  91.1 11.0 %collective-permute-start.7 = (bf16[64,1792]{1,0:T(8,128)(2,1)S(1)}, bf16[64,1792]{1,0:T(8,128)(2,1)S(1)}, u32[]{:S(2)}, u32[]{:S(2)}) collective-permute-start(bf16[64,1792]{1,0:T(8,128)(2,1)S(1)} %get-tuple-element.35), channel_id=1, source_target_pairs={{0,16},{1,17},{2,66},{3,67},{4,20},{5,21},{6,70},{7,71},{8,24},{9,... | collective-permute-start | bytes 688136 | tf_op jit(solution)/shard_map/ppermute | solution.py:28
  95.6 8.9 %collective-permute-start.8 = (bf16[64,1792]{1,0:T(8,128)(2,1)S(1)}, bf16[64,1792]{1,0:T(8,128)(2,1)S(1)}, u32[]{:S(2)}, u32[]{:S(2)}) collective-permute-start(bf16[64,1792]{1,0:T(8,128)(2,1)S(1)} %get-tuple-element.36), channel_id=1, source_target_pairs={{0,24},{1,25},{2,98},{3,99},{4,28},{5,29},{6,102},{7,103},{8,16},{... | collective-permute-start | bytes 688136 | tf_op jit(solution)/shard_map/ppermute | solution.py:28
  104.6 6.2 %collective-permute-start.9 = (bf16[64,1792]{1,0:T(8,128)(2,1)S(1)}, bf16[64,1792]{1,0:T(8,128)(2,1)S(1)}, u32[]{:S(2)}, u32[]{:S(2)}) collective-permute-start(bf16[64,1792]{1,0:T(8,128)(2,1)S(1)} %get-tuple-element.38), channel_id=1, source_target_pairs={{0,32},{1,33},{2,10},{3,11},{4,36},{5,37},{6,14},{7,15},{8,40},{9,... | collective-permute-start | bytes 688136 | tf_op jit(solution)/shard_map/ppermute | solution.py:28
  106.9 26.5 %collective-permute-start.21 = (bf16[2,256,1024]{2,1,0:T(8,128)(2,1)S(1)}, bf16[2,256,1024]{2,1,0:T(8,128)(2,1)S(1)}, u32[]{:S(2)}, u32[]{:S(2)}) collective-permute-start(bf16[2,256,1024]{2,1,0:T(8,128)(2,1)S(1)} %pad_maximum_fusion), channel_id=1, source_target_pairs={{0,96},{1,97},{2,26},{3,27},{4,100},{5,101},{6,30},{7,31},{8,104},... | collective-permute-start | bytes 3145736 | tf_op jit(solution)/shard_map/ppermute | solution.py:28
  110.1 18.7 %collective-permute-start.24 = (bf16[1792,256]{1,0:T(8,128)(2,1)S(1)}, bf16[1792,256]{1,0:T(8,128)(2,1)S(1)}, u32[]{:S(2)}, u32[]{:S(2)}) collective-permute-start(bf16[1792,256]{1,0:T(8,128)(2,1)S(1)} %dequant.1.refs_0_), channel_id=1, source_target_pairs={{0,2},{1,3},{2,0},{3,1},{4,6},{5,7},{6,4},{7,5},{8,10},{9,11},{10,... | collective-permute-start | bytes 2752520 | tf_op jit(solution)/shard_map/ppermute | solution.py:28
  110.1 18.7 %collective-permute-start.23 = (bf16[1792,256]{1,0:T(8,128)(2,1)}, bf16[1792,256]{1,0:T(8,128)(2,1)S(1)}, u32[]{:S(2)}, u32[]{:S(2)}) collective-permute-start(bf16[1792,256]{1,0:T(8,128)(2,1)} %collective-permute-done.16.refs_0_), channel_id=1, source_target_pairs={{0,2},{1,3},{2,0},{3,1},{4,6},{5,7},{6,4},{7,5},{8,10},{9,11},{10,... | collective-permute-start | bytes 2752520 | tf_op jit(solution)/shard_map/ppermute | solution.py:28
  110.6 7.6 %collective-permute-start.10 = (bf16[64,1792]{1,0:T(8,128)(2,1)S(1)}, bf16[64,1792]{1,0:T(8,128)(2,1)S(1)}, u32[]{:S(2)}, u32[]{:S(2)}) collective-permute-start(bf16[64,1792]{1,0:T(8,128)(2,1)S(1)} %get-tuple-element.39), channel_id=1, source_target_pairs={{0,64},{1,65},{2,18},{3,19},{4,68},{5,69},{6,22},{7,23},{8,72},{9,... | collective-permute-start | bytes 688136 | tf_op jit(solution)/shard_map/ppermute | solution.py:28
  110.8 17.1 %collective-permute-start.11 = (bf16[64,1792]{1,0:T(8,128)(2,1)S(1)}, bf16[64,1792]{1,0:T(8,128)(2,1)S(1)}, u32[]{:S(2)}, u32[]{:S(2)}) collective-permute-start(bf16[64,1792]{1,0:T(8,128)(2,1)S(1)} %get-tuple-element.40), channel_id=1, source_target_pairs={{0,96},{1,97},{2,26},{3,27},{4,100},{5,101},{6,30},{7,31},{8,104},... | collective-permute-start | bytes 688136 | tf_op jit(solution)/shard_map/ppermute | solution.py:28
  118.3 28.8 %collective-permute-start.22 = (bf16[1792,256]{1,0:T(8,128)(2,1)}, bf16[1792,256]{1,0:T(8,128)(2,1)}, u32[]{:S(2)}, u32[]{:S(2)}) collective-permute-start(bf16[1792,256]{1,0:T(8,128)(2,1)} %collective-permute-done.15.refs_0_), channel_id=1, source_target_pairs={{0,2},{1,3},{2,0},{3,1},{4,6},{5,7},{6,4},{7,5},{8,10},{9,11},{10,... | collective-permute-start | bytes 2752520 | tf_op jit(solution)/shard_map/ppermute | solution.py:28
  127.9 26.8 %collective-permute-start.18 = (bf16[1792,256]{1,0:T(8,128)(2,1)}, bf16[1792,256]{1,0:T(8,128)(2,1)}, u32[]{:S(2)}, u32[]{:S(2)}) collective-permute-start(bf16[1792,256]{1,0:T(8,128)(2,1)} %collective-permute-done.17.refs_0_), channel_id=1, source_target_pairs={{0,2},{1,3},{2,0},{3,1},{4,6},{5,7},{6,4},{7,5},{8,10},{9,11},{10,... | collective-permute-start | bytes 2752520 | tf_op jit(solution)/shard_map/ppermute | solution.py:28
  128.8 34.4 %collective-permute-start.12 = (bf16[64,1792]{1,0:T(8,128)(2,1)}, bf16[64,1792]{1,0:T(8,128)(2,1)S(1)}, u32[]{:S(2)}, u32[]{:S(2)}) collective-permute-start(bf16[64,1792]{1,0:T(8,128)(2,1)} %get-tuple-element.42), channel_id=1, source_target_pairs={{0,32},{1,33},{2,10},{3,11},{4,36},{5,37},{6,14},{7,15},{8,40},{9,... | collective-permute-start | bytes 688136 | tf_op jit(solution)/shard_map/ppermute | solution.py:28
  128.8 34.4 %collective-permute-start.13 = (bf16[64,1792]{1,0:T(8,128)(2,1)S(1)}, bf16[64,1792]{1,0:T(8,128)(2,1)S(1)}, u32[]{:S(2)}, u32[]{:S(2)}) collective-permute-start(bf16[64,1792]{1,0:T(8,128)(2,1)S(1)} %get-tuple-element.43), channel_id=1, source_target_pairs={{0,64},{1,65},{2,18},{3,19},{4,68},{5,69},{6,22},{7,23},{8,72},{9,... | collective-permute-start | bytes 688136 | tf_op jit(solution)/shard_map/ppermute | solution.py:28
  133.5 29.8 %collective-permute-start.14 = (bf16[64,1792]{1,0:T(8,128)(2,1)S(1)}, bf16[64,1792]{1,0:T(8,128)(2,1)S(1)}, u32[]{:S(2)}, u32[]{:S(2)}) collective-permute-start(bf16[64,1792]{1,0:T(8,128)(2,1)S(1)} %get-tuple-element.44), channel_id=1, source_target_pairs={{0,96},{1,97},{2,26},{3,27},{4,100},{5,101},{6,30},{7,31},{8,104},... | collective-permute-start | bytes 688136 | tf_op jit(solution)/shard_map/ppermute | solution.py:28
  (12 other events, 221.8 us)

commit v2 on v1

v2 whole, which is shorter than its diff:
```python
import functools
import math

import jax
import jax.numpy as jnp
from jax import lax
from jax.experimental import pallas as pl
from jax.experimental.pallas import tpu as pltpu
from jax.sharding import PartitionSpec as P


BLOCK = 128
TILE = 256
PARTS = ((0, 1024), (1024, 768))
AXES = ("hid", "wid", "rep")
F32 = jnp.float32
BF16 = jnp.bfloat16
ANY_SPEC = pl.BlockSpec(memory_space=pl.ANY)
VMEM_SPEC = pl.BlockSpec(memory_space=pltpu.VMEM)
SMALL = pltpu.CompilerParams(vmem_limit_bytes=12 << 20)


def send(value, target):
    route = []
    for hid in range(16):
        for wid in range(4):
            for rep in range(2):
                to_hid, to_wid, to_rep = target(hid, wid, rep)
                route.append((hid * 8 + wid * 2 + rep, to_hid * 8 + to_wid * 2 + to_rep))
    return lax.ppermute(value, AXES, route)


def to_mate(hid, wid, rep):
    return hid, wid ^ 1, rep


def to_pair(hid, wid, rep):
    return hid, wid ^ 2, rep


def to_next(hid, wid, rep):
    return hid, wid ^ 2, rep ^ 1


def to_rep(hid, wid, rep):
    return hid, wid, rep ^ 1


def along(axis, step):
    return lambda hid, wid, rep: (hid ^ (step << 2 * ((wid & 1) ^ axis)), wid, rep)


def place(axis):
    hid = lax.axis_index("hid")
    return jnp.where(lax.axis_index("wid") & 1 == axis, hid, hid >> 2) & 3


def dequant_kernel(codes_ref, exponents_ref, out_ref):
    step = pl.program_id(0)
    blocks = codes_ref.shape[1] // BLOCK
    for half in range(blocks):
        drop = -exponents_ref[step * blocks + half]
        scale = jnp.where(drop & 1 == 1, 0.5, 1.0) * jnp.where(drop & 2 == 2, 0.25, 1.0)
        scale = scale * jnp.where(drop & 4 == 4, 2.0 ** -4, 1.0) * jnp.where(drop & 8 == 8, 2.0 ** -8, 1.0)
        span = pl.ds(half * BLOCK, BLOCK)
        out_ref[pl.ds(pl.multiple_of((step * blocks + half) * BLOCK, BLOCK), BLOCK), :] = (codes_ref[:, span].astype(F32).T * scale).astype(BF16)


def dequant_t(codes, exponents_t):
    tokens, hidden = codes.shape
    tile = hidden // 2
    return pl.pallas_call(
        dequant_kernel,
        out_shape=pltpu.VMEM((hidden, tokens), BF16),
        grid=(hidden // tile,),
        in_specs=[pl.BlockSpec((tokens, tile), lambda i: (0, i)), pl.BlockSpec(exponents_t.shape, lambda i: (0, 0, 0))],
        out_specs=pl.BlockSpec(memory_space=pltpu.VMEM),
        compiler_params=pltpu.CompilerParams(vmem_limit_bytes=12 << 20),
        name="dequant",
    )(codes, exponents_t)


CONTRACT = (((1,), (1,)), ((), ()))


def scatter_rows(total_ref, outs, first):
    tokens = outs[0].shape[0]
    wid = lax.axis_index("wid")
    cols = pl.ds(pl.multiple_of(first, TILE), TILE)
    for flip, out in zip((3, 2, 1, 0), outs):
        out[:, cols] = total_ref[pl.ds(pl.multiple_of((wid ^ flip) * tokens, tokens), tokens), :]


def first_product_kernel(rows_ref, w_ref, *refs):
    outs, (rows_out, w_out, w_buf, total_ref, rows_sem, w_sem, rest_sem) = refs[:4], refs[4:]
    count = outs[0].shape[1]
    chunk = rows_ref.shape[0] // 4

    def weights(tile):
        span = pl.ds(pl.multiple_of(tile * TILE, TILE), TILE)
        return pltpu.make_async_copy(w_ref.at[span], w_buf.at[span], w_sem.at[tile])

    rows = [pltpu.make_async_copy(rows_ref.at[pl.ds(i * chunk, chunk)], rows_out.at[pl.ds(i * chunk, chunk)], rows_sem.at[i])
            for i in range(4)]
    rest = pltpu.make_async_copy(w_ref.at[pl.ds(count, w_out.shape[0])], w_out, rest_sem)
    weights(0).start()
    for copy in rows:
        copy.start()
    for tile in range(1, count // TILE):
        weights(tile).start()
    rest.start()
    for copy in rows:
        copy.wait()

    def body(tile, carry):
        weights(tile).wait()
        span = pl.ds(pl.multiple_of(tile * TILE, TILE), TILE)
        total_ref[...] = lax.dot_general(
            rows_out[...], w_buf[span, :], CONTRACT, preferred_element_type=F32).astype(BF16)
        scatter_rows(total_ref, outs, tile * TILE)
        return carry

    lax.fori_loop(0, count // TILE, body, 0)
    rest.wait()


def first_product(rows, weight, count):
    total, width = rows.shape
    hbm = pl.BlockSpec(memory_space=pltpu.HBM)
    return pl.pallas_call(
        first_product_kernel,
        out_shape=[pltpu.VMEM((total // 4, count), BF16)] * 4
        + [pltpu.VMEM((total, width), BF16), pltpu.VMEM((weight.shape[0] - count, width), BF16)],
        in_specs=[hbm, hbm],
        out_specs=[VMEM_SPEC] * 6,
        scratch_shapes=[pltpu.VMEM((count, width), BF16), pltpu.VMEM((total, TILE), BF16), pltpu.SemaphoreType.DMA((4,)),
                        pltpu.SemaphoreType.DMA((count // TILE,)), pltpu.SemaphoreType.DMA(())],
        compiler_params=pltpu.CompilerParams(vmem_limit_bytes=52 << 20),
        name="first_product",
    )(rows, weight)


def second_product_kernel(rows_ref, w_ref, *refs):
    outs, total_ref = refs[:4], refs[4]

    def body(tile, carry):
        span = pl.ds(pl.multiple_of(tile * TILE, TILE), TILE)
        total_ref[...] = lax.dot_general(
            rows_ref[...], w_ref[span, :], CONTRACT, preferred_element_type=F32).astype(BF16)
        scatter_rows(total_ref, outs, tile * TILE)
        return carry

    lax.fori_loop(0, outs[0].shape[1] // TILE, body, 0)


def second_product(rows, weight):
    total, count = rows.shape[0], weight.shape[0]
    return pl.pallas_call(
        second_product_kernel,
        out_shape=[pltpu.VMEM((total // 4, count), BF16)] * 4,
        in_specs=[VMEM_SPEC] * 2,
        out_specs=[VMEM_SPEC] * 4,
        scratch_shapes=[pltpu.VMEM((total, TILE), BF16)],
        compiler_params=SMALL,
        name="second_product",
    )(rows, weight)


def small(kernel, operands, shape, spec=None):
    return pl.pallas_call(
        kernel,
        out_shape=pltpu.VMEM(shape, BF16),
        in_specs=[spec or VMEM_SPEC] * len(operands),
        out_specs=VMEM_SPEC,
        scratch_shapes=[pltpu.SemaphoreType.DMA(())] if spec else [],
        compiler_params=pltpu.CompilerParams(vmem_limit_bytes=60 << 20) if spec else SMALL,
    )(*operands)


def quarter_kernel(rows_ref, out_ref, sem):
    hid = lax.axis_index("hid")
    tokens, half = out_ref.shape
    quarter = ((hid >> 2) & 1) * 2 + (hid & 1)
    source = rows_ref.at[pl.ds(pl.multiple_of(quarter * tokens, tokens), tokens),
                         pl.ds(pl.multiple_of((1 - lax.axis_index("rep")) * half, half), half)]
    copy = pltpu.make_async_copy(source, out_ref, sem)
    copy.start()
    copy.wait()


def join_kernel(a_ref, b_ref, out_ref):
    out_ref[...] = (a_ref[...].astype(F32) + b_ref[...].astype(F32)).astype(BF16)


def stack_kernel(a_ref, b_ref, out_ref):
    out_ref[0] = a_ref[...]
    out_ref[1] = b_ref[...]


def choose_kernel(a_ref, b_ref, out_ref):
    core = lax.axis_index("wid") & 1
    for number, source in enumerate((a_ref, b_ref)):
        @pl.when(core == number)
        def _():
            out_ref[...] = source[...]


def rotate_kernel(*refs, scale, parts):
    codes_ref = refs[3 * len(parts)]
    outs, mixed_ref = refs[3 * len(parts) + 1:-1], refs[-1]
    rows = outs[0].shape[0]
    mine = place(0)
    row = lax.broadcasted_iota(jnp.int32, (TILE, TILE), 0)
    col = lax.broadcasted_iota(jnp.int32, (TILE, TILE), 1)
    bits = row & col & (BLOCK - 1)
    for shift in (4, 2, 1):
        bits = bits ^ (bits >> shift)
    sign = (1 - 2 * (bits & 1)).astype(F32)
    table = jnp.where((row ^ col) < BLOCK, sign, 0.0).astype(BF16)
    for part, (start, count) in enumerate(parts):
        keep_ref, away_ref, far_ref = refs[3 * part:3 * part + 3]
        for first in range(0, count, TILE):
            here = pl.ds(first, TILE)
            cols = pl.ds(start + first, TILE)
            total = keep_ref[:, here].astype(F32) + away_ref[:, here].astype(F32) + far_ref[:, here].astype(F32)
            codes = codes_ref[:, cols]
            masked = jnp.where((codes > -128) & (codes < 127), total, 0.0).astype(BF16)
            mixed = jnp.dot(masked, table, preferred_element_type=F32)
            mixed_ref[:, cols] = (mixed * scale).astype(BF16)
    for step, out in enumerate(outs):
        out[...] = mixed_ref[pl.ds(pl.multiple_of((mine ^ step) * rows, rows), rows), :]


def rotate(sums, codes, scale):
    tokens, hidden = codes.shape
    return pl.pallas_call(
        functools.partial(rotate_kernel, scale=scale, parts=PARTS),
        out_shape=[pltpu.VMEM((tokens // 4, hidden), BF16)] * 4,
        in_specs=[VMEM_SPEC] * (3 * len(PARTS) + 1),
        out_specs=[VMEM_SPEC] * 4,
        scratch_shapes=[pltpu.VMEM((tokens, hidden), BF16)],
        compiler_params=SMALL,
        name="rotate",
    )(*[value for group in sums for value in group], codes)


def parity(value):
    return (1 - 2 * ((value ^ (value >> 1)) & 1)).astype(F32)


def mix_kernel(*refs, axis):
    mine = place(axis)
    signs = [parity(mine & step) for step in range(4)]
    whole = parity(mine)
    hidden = refs[0].shape[1]
    for first in range(0, hidden, TILE):
        cols = pl.ds(first, TILE)
        p0, p1, p2, p3 = [refs[step][:, cols].astype(F32) * signs[step] for step in range(4)]
        even, odd = (p0 + p1, p2 + p3), (p0 - p1, p2 - p3)
        outs = (even[0] + even[1], odd[0] + odd[1], even[0] - even[1], odd[0] - odd[1])
        for step in range(4):
            refs[4 + step][:, cols] = (outs[step] * (whole * signs[step])).astype(BF16)


def relabel_kernel(*refs):
    turn = place(0) ^ place(1)
    for step in range(4):
        for other in range(4):
            @pl.when(turn == step ^ other)
            def _():
                refs[4 + step][...] = refs[other][...]


def four(kernel, pieces):
    return pl.pallas_call(
        kernel,
        out_shape=[pltpu.VMEM(pieces[0].shape, BF16)] * 4,
        in_specs=[VMEM_SPEC] * 4,
        out_specs=[VMEM_SPEC] * 4,
        compiler_params=SMALL,
    )(*pieces)


def finish_kernel(p0, p1, p2, p3, gate_ref, up_ref, gate_out, up_out):
    mine = place(1)
    rows = p0.shape[0]
    for step, piece in enumerate((p0, p1, p2, p3)):
        span = pl.ds(pl.multiple_of((mine ^ step) * rows, rows), rows)
        for first in range(0, piece.shape[1], TILE):
            cols = pl.ds(first, TILE)
            hidden = piece[:, cols].astype(F32)
            gate = gate_ref[span, cols].astype(F32)
            up = up_ref[span, cols].astype(F32)
            sig = jax.nn.sigmoid(gate)
            gate_out[span, cols] = (hidden * up * sig * (1.0 + gate * (1.0 - sig))).astype(BF16)
            up_out[span, cols] = (hidden * gate * sig).astype(BF16)


def finish(pieces, gate, up):
    return pl.pallas_call(
        finish_kernel,
        out_shape=[jax.ShapeDtypeStruct(gate.shape, BF16)] * 2,
        in_specs=[VMEM_SPEC] * 6,
        out_specs=[VMEM_SPEC] * 2,
        compiler_params=SMALL,
        name="finish",
    )(*pieces, gate, up)


def arrange_kernel(g0, g1, g23, out_ref):
    hid = lax.axis_index("hid")
    core = lax.axis_index("wid") & 1
    quarter = ((hid >> 2) & 1) * 2 + (hid & 1)
    tokens = g0.shape[0]
    for source, flip in ((g0, 0), (g1, 1 + core), (g23.at[0], 2 - core), (g23.at[1], 3)):
        out_ref[pl.ds(pl.multiple_of((quarter ^ flip) * tokens, tokens), tokens), :] = source[...]


def arrange(g0, g1, g23):
    return pl.pallas_call(
        arrange_kernel,
        out_shape=pltpu.VMEM((4 * g0.shape[0], g0.shape[1]), BF16),
        in_specs=[VMEM_SPEC] * 3,
        out_specs=VMEM_SPEC,
        compiler_params=SMALL,
        name="arrange",
    )(g0, g1, g23)


def down_kernel(*refs, flips, summed, last, mine):
    count = len(flips)
    pieces, rows_ref = refs[:count], refs[count]
    acc_ref = refs[count + 1] if summed else None
    out_ref = refs[count + 1 + summed]
    wid = lax.axis_index("wid")
    tokens = pieces[0].shape[1]
    width = out_ref.shape[1]
    offset = lax.axis_index("rep") * width if mine else 0
    copies = []
    for number, first in enumerate(range(0, width, TILE)):
        cols = pl.ds(first, TILE)
        total = None
        for piece, flip in zip(pieces, flips):
            right = rows_ref[pl.ds(pl.multiple_of((wid ^ flip) * tokens, tokens), tokens),
                             pl.ds(pl.multiple_of(offset + first, TILE), TILE)]
            part = jnp.dot(piece[...], right, preferred_element_type=F32)
            total = part if total is None else total + part
        if summed:
            total = total + acc_ref[:, cols].astype(F32)
        if not last:
            out_ref[:, cols] = total.astype(BF16)
            continue
        buffer_ref, sem = refs[-2:]
        buffer_ref[number] = total
        copies.append(pltpu.make_async_copy(buffer_ref.at[number], out_ref.at[:, cols], sem.at[number]))
        copies[-1].start()
    for copy in copies:
        copy.wait()


def down(pieces, flips, rows, width, acc=None, last=False):
    hidden, _ = pieces[0].shape
    operands = (*pieces, rows) if acc is None else (*pieces, rows, acc)
    scratch = [pltpu.VMEM((width // TILE, hidden, TILE), F32), pltpu.SemaphoreType.DMA((width // TILE,))]
    return pl.pallas_call(
        functools.partial(
            down_kernel, flips=flips, summed=acc is not None, last=last, mine=rows.shape[1] > width),
        out_shape=jax.ShapeDtypeStruct((hidden, width), F32) if last else pltpu.VMEM((hidden, width), BF16),
        in_specs=[VMEM_SPEC] * len(operands),
        out_specs=ANY_SPEC if last else VMEM_SPEC,
        scratch_shapes=scratch if last else [],
        compiler_params=pltpu.CompilerParams(vmem_limit_bytes=24 << 20),
        name="down",
    )(*operands)


def shards(grad_out, down_weight, saved_gate, saved_up, saved_codes, exponents):
    rows = grad_out[0]
    codes = saved_codes[0]
    tokens = codes.shape[0]
    half = rows.shape[1] // 2
    scale = 1.0 / math.sqrt(BLOCK * 16)

    g0 = small(quarter_kernel, (rows,), (tokens, half), pl.BlockSpec(memory_space=pltpu.HBM))
    g0 = send(g0, to_rep)
    g1 = send(g0, lambda h, w, r: (h ^ (3 if w & 1 == 0 else 12), w, r))
    g23 = small(stack_kernel, (g0, g1), (2, tokens, half))
    g23 = send(g23, lambda h, w, r: (h ^ (12 if w & 1 == 0 else 3), w, r))

    own = dequant_t(codes, jnp.transpose(exponents, (2, 0, 1)))
    own_mate = send(own, to_mate)
    next_ = send(own, to_next)
    next_mate = send(next_, to_mate)

    sums = []
    for part, (first, count) in enumerate(PARTS):
        if part == 0:
            far_away, far_keep, near_away, near_keep, rows_near, rest = first_product(rows, down_weight, count)
        else:
            far_away, far_keep, near_away, near_keep = second_product(rows_near, rest)
        far_away = send(far_away, to_mate)
        near_away = send(near_away, to_mate)
        far = small(join_kernel, (far_keep, far_away), far_keep.shape)
        far = send(far, to_pair)
        sums.append((near_keep, near_away, far))

    pair = send(own, to_pair)
    pair_mate = send(pair, to_mate)
    cross = small(choose_kernel, (pair, next_), pair.shape)
    cross = send(cross, lambda h, w, r: (h, w ^ 2, r ^ 1 if w & 1 == 0 else r))
    cross_mate = send(cross, to_mate)

    product = down((own, own_mate), (0, 1), rows_near, half)
    other_rows = arrange(g0, g1, g23)
    product = down((next_, next_mate), (2, 3), other_rows, half, product)
    product = down((pair, pair_mate), (2, 3), rows_near, half, product)

    def spread(pieces, axis):
        moved = list(pieces)
        for step in (2, 1, 3):
            moved[step] = send(pieces[step], along(axis, step))
        return moved

    pieces = rotate(sums, codes, scale)
    pieces = spread(pieces, 0)
    pieces = four(functools.partial(mix_kernel, axis=0), pieces)
    pieces = spread(pieces, 0)
    pieces = four(relabel_kernel, pieces)
    pieces = spread(pieces, 1)
    pieces = four(functools.partial(mix_kernel, axis=1), pieces)
    pieces = spread(pieces, 1)
    grad_gate, grad_up = finish(pieces, saved_gate[0], saved_up[0])

    grad_down = down((cross, cross_mate), (0, 1), other_rows, half, product, last=True)
    return grad_gate[None], grad_up[None], grad_down


def solution(mesh):
    in_specs = (
        P("rep", None, "wid"),
        P("hid", "wid"),
        P("rep", "wid", "hid"),
        P("rep", "wid", "hid"),
        P("rep", "wid", "hid"),
        P("rep", "wid", "hid"),
    )
    out_specs = (P("rep", "wid", "hid"), P("rep", "wid", "hid"), P("hid", ("wid", "rep")))


    return jax.shard_map(shards, mesh=mesh, in_specs=in_specs, out_specs=out_specs, check_vma=False)
```

time: 167 us -> 150 us (0.90)
  Pallas kernels: 50.1 us -> 36.8 us
  starting transfers between devices: 34.8 us -> 26.4 us
  local copies, waits for them, and re-layouts: 3.09 us -> 7.83 us
  waiting for transfers between devices: 72.8 us -> 77.5 us
  other arithmetic: 3.72 us -> 0 us
    pallas_call x6 -> x13, Pallas kernels: 43.2 us -> 31.8 us  [the longest x4 12.9 us: down(): pl.pallas_call(functools.partial(down_kernel, flips=flips, summed=acc is...]
    ppermute x25 -> x28, starting transfers between devices: 34.8 us -> 26.4 us  [send(): return lax.ppermute(value, AXES, route)]
    unnamed x22 -> x24, local copies, waits for them, and re-layouts: 1.22 us -> 7.83 us
    ppermute x25 -> x28, waiting for transfers between devices: 72.8 us -> 77.5 us  [send(): return lax.ppermute(value, AXES, route)]
    convert_element_type x1 -> x0, other arithmetic: 2.35 us -> none  [shards(): far = (far_keep.astype(F32) + far_away.astype(F32)).astype(BF16)]
    dynamic_slice x1 -> x0, local copies, waits for them, and re-layouts: 1.87 us -> none  [shards(): lax.dynamic_slice(rows, (quarter * tokens, (1 - rep) * half), (tokens, ha...]
  transfers between devices with their start and end apart: 25 -> 28, of which waited for: 12 -> 11; matrix products, arithmetic and copies ran while one was open for 3% -> 0% of each run, Pallas kernels for 21% -> 15%
where the time goes in v2:
time: 150 us; the launch traced here: 149 us
  waiting for transfers between devices  77.5 us (52%)
  Pallas kernels  36.8 us (25%)
  starting transfers between devices  26.4 us (18%)
  local copies, waits for them, and re-layouts  7.83 us (5%)
    ppermute x28, waiting for transfers between devices, send(): return lax.ppermute(value, AXES, route)  77.5 us
    ppermute x28, starting transfers between devices, send(): return lax.ppermute(value, AXES, route)  26.4 us
    pallas_call x4, Pallas kernels, down(): pl.pallas_call(functools.partial(down_kernel, flips=flips, summed=acc is...  12.9 us
    pallas_call x1, Pallas kernels, first_product(): pl.pallas_call(first_product_kernel, out_shape=[pltpu.VMEM((total // 4, c...  9.41 us
    unnamed x24, local copies, waits for them, and re-layouts  7.83 us
    pallas_call x5, Pallas kernels, small(): pl.pallas_call(kernel, out_shape=pltpu.VMEM(shape, BF16), in_specs=[spec...  4.57 us
    pallas_call x1, Pallas kernels, second_product(): pl.pallas_call(second_product_kernel, out_shape=[pltpu.VMEM((total // 4,...  3.98 us
  transfers between devices with their start and end apart: 28, of which 11 were waited for; matrix products, arithmetic and copies ran while one was open for 0% of the time, Pallas kernels for 15%

profile of v2, /device:TPU:0, one launch (start us, length us, event | category | flops | bytes accessed | tf_op | source)
XLA Modules:
  0.0 149.5 jit_solution(436615919382094186)
XLA Ops:
  0.6 9.4 %first_product.1 = (bf16[256,1024]{1,0:T(8,128)(2,1)S(1)}, bf16[256,1024]{1,0:T(8,128)(2,1)S(1)}, bf16[256,1024]{1,0:T(8,128)(2,1)}, bf16[256,1024]{1,0:T(8,128)...) custom-call(bf16[1024,2048]{1,0:T(8,128)(2,1)} %bitcast.12, bf16[1792,2048]{1,0:T(8,128)(2,1)} %w_ref.1), custom_call_target="tpu_custom_call" | custom-call | tf_op jit(solution)/shard_map/first_product/pallas_call | solution.py:130
  11.7 3.4 %copy-done.4 = bf16[768,2048]{1,0:T(8,128)(2,1)S(1)} copy-done((bf16[768,2048]{1,0:T(8,128)(2,1)S(1)}, bf16[768,2048]{1,0:T(8,128)(2,1)}, u32[]{:S(2)}) %copy-start.4) | copy-done | bytes 3145752
  15.1 4.0 %second_product.1 = (bf16[256,768]{1,0:T(8,128)(2,1)S(1)}, bf16[256,768]{1,0:T(8,128)(2,1)S(1)}, bf16[256,768]{1,0:T(8,128)(2,1)S(1)}, bf16[256,768]{1,0:T(8,128)(2,1)S(1)}) custom-call(bf16[1024,2048]{1,0:T(8,128)(2,1)S(1)} %get-tuple-element.35.rows_ref.refs_2_, bf16[768,2048]{1,0:T(8,128)(2,1)S(1)} %copy-done.4), custom_call_target="tpu_custom_call" | custom-call | tf_op jit(solution)/shard_map/second_product/pallas_call | solution.py:158
  20.0 4.2 %collective-permute-start.19 = (bf16[1792,256]{1,0:T(8,128)(2,1)S(1)}, bf16[1792,256]{1,0:T(8,128)(2,1)}, u32[]{:S(2)}, u32[]{:S(2)}) collective-permute-start(bf16[1792,256]{1,0:T(8,128)(2,1)S(1)} %dequant.1.refs_0_), channel_id=1, source_target_pairs={{0,5},{1,4},{2,7},{3,6},{4,1},{5,0},{6,3},{7,2},{8,13},{9,12},{10,... | collective-permute-start | bytes 2752520 | tf_op jit(solution)/shard_map/ppermute | solution.py:30
  32.0 35.4 %collective-permute-done.5.refs_5_ = bf16[256,768]{1,0:T(8,128)(2,1)} collective-permute-done((bf16[256,768]{1,0:T(8,128)(2,1)}, bf16[256,768]{1,0:T(8,128)(2,1)}, u32[]{:S(2)}, u32[]{:S(2)}) %collective-permute-start.5) | collective-permute-done | bytes 393248 | tf_op jit(solution)/shard_map/ppermute | solution.py:30
  69.4 2.1 %rotate.1 = (bf16[64,1792]{1,0:T(8,128)(2,1)S(1)}, bf16[64,1792]{1,0:T(8,128)(2,1)S(1)}, bf16[64,1792]{1,0:T(8,128)(2,1)S(1)}, bf16[64,1792]{1,0:T(8,128)(2,1)S(1)}) custom-call(bf16[256,1024]{1,0:T(8,128)(2,1)S(1)} %get-tuple-element.31.refs_0_, bf16[256,1024]{1,0:T(8,128)(2,1)} %collective-permute-done.refs_1_, ...), custom_call_target="tpu_custom_call" | custom-call | tf_op jit(solution)/shard_map/rotate/pallas_call | solution.py:236
  73.2 2.9 %collective-permute-start.7 = (bf16[64,1792]{1,0:T(8,128)(2,1)S(1)}, bf16[64,1792]{1,0:T(8,128)(2,1)S(1)}, u32[]{:S(2)}, u32[]{:S(2)}) collective-permute-start(bf16[64,1792]{1,0:T(8,128)(2,1)S(1)} %get-tuple-element.43), channel_id=1, source_target_pairs={{0,16},{1,17},{2,66},{3,67},{4,20},{5,21},{6,70},{7,71},{8,24},{9,... | collective-permute-start | bytes 688136 | tf_op jit(solution)/shard_map/ppermute | solution.py:30
  78.5 4.2 %collective-permute-done.7.refs_2_ = bf16[64,1792]{1,0:T(8,128)(2,1)S(1)} collective-permute-done((bf16[64,1792]{1,0:T(8,128)(2,1)S(1)}, bf16[64,1792]{1,0:T(8,128)(2,1)S(1)}, u32[]{:S(2)}, u32[]{:S(2)}) %collective-permute-start.7) | collective-permute-done | bytes 229408 | tf_op jit(solution)/shard_map/ppermute | solution.py:30
  82.7 2.4 %collective-permute-done.8.refs_3_ = bf16[64,1792]{1,0:T(8,128)(2,1)S(1)} collective-permute-done((bf16[64,1792]{1,0:T(8,128)(2,1)S(1)}, bf16[64,1792]{1,0:T(8,128)(2,1)S(1)}, u32[]{:S(2)}, u32[]{:S(2)}) %collective-permute-start.8) | collective-permute-done | bytes 229408 | tf_op jit(solution)/shard_map/ppermute | solution.py:30
  85.6 2.2 %collective-permute-start.23 = (bf16[256,1024]{1,0:T(8,128)(2,1)S(1)}, bf16[256,1024]{1,0:T(8,128)(2,1)S(1)}, u32[]{:S(2)}, u32[]{:S(2)}) collective-permute-start(bf16[256,1024]{1,0:T(8,128)(2,1)S(1)} %collective-permute-done.22.a_ref.g0), channel_id=1, source_target_pairs={{0,24},{1,25},{2,98},{3,99},{4,28},{5,29},{6,102},{7,103},{8,16},{... | collective-permute-start | bytes 1572872 | tf_op jit(solution)/shard_map/ppermute | solution.py:30
  88.9 4.2 %collective-permute-done.10.refs_2_ = bf16[64,1792]{1,0:T(8,128)(2,1)S(1)} collective-permute-done((bf16[64,1792]{1,0:T(8,128)(2,1)S(1)}, bf16[64,1792]{1,0:T(8,128)(2,1)S(1)}, u32[]{:S(2)}, u32[]{:S(2)}) %collective-permute-start.10) | collective-permute-done | bytes 229408 | tf_op jit(solution)/shard_map/ppermute | solution.py:30
  93.1 7.9 %collective-permute-done.11.refs_3_ = bf16[64,1792]{1,0:T(8,128)(2,1)S(1)} collective-permute-done((bf16[64,1792]{1,0:T(8,128)(2,1)S(1)}, bf16[64,1792]{1,0:T(8,128)(2,1)S(1)}, u32[]{:S(2)}, u32[]{:S(2)}) %collective-permute-start.11) | collective-permute-done | bytes 229408 | tf_op jit(solution)/shard_map/ppermute | solution.py:30
  102.6 2.7 %collective-permute-start.13 = (bf16[64,1792]{1,0:T(8,128)(2,1)S(1)}, bf16[64,1792]{1,0:T(8,128)(2,1)S(1)}, u32[]{:S(2)}, u32[]{:S(2)}) collective-permute-start(bf16[64,1792]{1,0:T(8,128)(2,1)S(1)} %get-tuple-element.51), channel_id=1, source_target_pairs={{0,64},{1,65},{2,18},{3,19},{4,68},{5,69},{6,22},{7,23},{8,72},{9,... | collective-permute-start | bytes 688136 | tf_op jit(solution)/shard_map/ppermute | solution.py:30
  107.2 2.7 %collective-permute-start.24 = (bf16[2,256,1024]{2,1,0:T(8,128)(2,1)S(1)}, bf16[2,256,1024]{2,1,0:T(8,128)(2,1)S(1)}, u32[]{:S(2)}, u32[]{:S(2)}) collective-permute-start(bf16[2,256,1024]{2,1,0:T(8,128)(2,1)S(1)} %shard_map.92), channel_id=1, source_target_pairs={{0,96},{1,97},{2,26},{3,27},{4,100},{5,101},{6,30},{7,31},{8,104},... | collective-permute-start | bytes 3145736 | tf_op jit(solution)/shard_map/ppermute | solution.py:30
  109.9 2.0 %collective-permute-done.13.refs_2_ = bf16[64,1792]{1,0:T(8,128)(2,1)S(1)} collective-permute-done((bf16[64,1792]{1,0:T(8,128)(2,1)S(1)}, bf16[64,1792]{1,0:T(8,128)(2,1)S(1)}, u32[]{:S(2)}, u32[]{:S(2)}) %collective-permute-start.13) | collective-permute-done | bytes 229408 | tf_op jit(solution)/shard_map/ppermute | solution.py:30
  111.9 2.4 %collective-permute-done.14.refs_3_ = bf16[64,1792]{1,0:T(8,128)(2,1)S(1)} collective-permute-done((bf16[64,1792]{1,0:T(8,128)(2,1)S(1)}, bf16[64,1792]{1,0:T(8,128)(2,1)S(1)}, u32[]{:S(2)}, u32[]{:S(2)}) %collective-permute-start.14) | collective-permute-done | bytes 229408 | tf_op jit(solution)/shard_map/ppermute | solution.py:30
  115.4 6.0 %collective-permute-done.15.p1 = bf16[64,1792]{1,0:T(8,128)(2,1)S(1)} collective-permute-done((bf16[64,1792]{1,0:T(8,128)(2,1)S(1)}, bf16[64,1792]{1,0:T(8,128)(2,1)S(1)}, u32[]{:S(2)}, u32[]{:S(2)}) %collective-permute-start.15) | collective-permute-done | bytes 229408 | tf_op jit(solution)/shard_map/ppermute | solution.py:30
  121.8 7.1 %collective-permute-done.16.p2 = bf16[64,1792]{1,0:T(8,128)(2,1)S(1)} collective-permute-done((bf16[64,1792]{1,0:T(8,128)(2,1)S(1)}, bf16[64,1792]{1,0:T(8,128)(2,1)S(1)}, u32[]{:S(2)}, u32[]{:S(2)}) %collective-permute-start.16) | collective-permute-done | bytes 229408 | tf_op jit(solution)/shard_map/ppermute | solution.py:30
  129.4 2.1 %down.4.refs_3_ = bf16[1792,1024]{1,0:T(8,128)(2,1)S(1)} custom-call(bf16[1792,256]{1,0:T(8,128)(2,1)S(1)} %dequant.1.refs_0_, bf16[1792,256]{1,0:T(8,128)(2,1)S(1)} %collective-permute-done.27.refs_1_, bf16[1024,2048]{1,0:T(8,128)(2,1)S(1)} %copy-done.1), custom_call_target="tpu_custom_call" | custom-call | tf_op jit(solution)/shard_map/down/pallas_call | solution.py:365
  131.5 4.6 %collective-permute-done.17.p3 = bf16[64,1792]{1,0:T(8,128)(2,1)S(1)} collective-permute-done((bf16[64,1792]{1,0:T(8,128)(2,1)S(1)}, bf16[64,1792]{1,0:T(8,128)(2,1)S(1)}, u32[]{:S(2)}, u32[]{:S(2)}) %collective-permute-start.17) | collective-permute-done | bytes 229408 | tf_op jit(solution)/shard_map/ppermute | solution.py:30
  136.2 2.1 %finish.1 = (bf16[256,1792]{1,0:T(8,128)(2,1)}, bf16[256,1792]{1,0:T(8,128)(2,1)}) custom-call(bf16[64,1792]{1,0:T(8,128)(2,1)S(1)} %get-tuple-element.53.p0, bf16[64,1792]{1,0:T(8,128)(2,1)S(1)} %collective-permute-done.15.p1, bf16[64,1792]{1,0:T(8,128)(2,1)S(1)} %collective-permute-done.16.p2, bf16[64,1792]{1,0:T(8,128)(2,1)S(1)} %collective-permute-done.17.p3, ...), custom_call_target="tpu_custom_call" | custom-call | tf_op jit(solution)/shard_map/finish/pallas_call | solution.py:300
  138.5 3.2 %down.5.refs_3_ = bf16[1792,1024]{1,0:T(8,128)(2,1)S(1)} custom-call(bf16[1792,256]{1,0:T(8,128)(2,1)} %collective-permute-done.19.b_ref.refs_0_, bf16[1792,256]{1,0:T(8,128)(2,1)S(1)} %collective-permute-done.26.refs_1_, bf16[1024,1024]{1,0:T(8,128)(2,1)S(1)} %arrange.1.refs_2_, bf16[1792,1024]{1,0:T(8,128)(2,1)S(1)} %down.4.refs_3_), custom_call_target="tpu_custom_call" | custom-call | tf_op jit(solution)/shard_map/down/pallas_call | solution.py:365
  141.8 3.3 %down.6.refs_3_ = bf16[1792,1024]{1,0:T(8,128)(2,1)S(1)} custom-call(bf16[1792,256]{1,0:T(8,128)(2,1)} %collective-permute-done.18.a_ref.refs_0_, bf16[1792,256]{1,0:T(8,128)(2,1)S(1)} %collective-permute-done.25.refs_1_, bf16[1024,2048]{1,0:T(8,128)(2,1)S(1)} %copy-done.1, bf16[1792,1024]{1,0:T(8,128)(2,1)S(1)} %down.5.refs_3_), custom_call_target="tpu_custom_call" | custom-call | tf_op jit(solution)/shard_map/down/pallas_call | solution.py:365
  145.0 4.3 %down.7 = f32[1792,1024]{1,0:T(8,128)} custom-call(bf16[1792,256]{1,0:T(8,128)(2,1)S(1)} %collective-permute-done.20.refs_0_, bf16[1792,256]{1,0:T(8,128)(2,1)S(1)} %collective-permute-done.21.refs_1_, bf16[1024,1024]{1,0:T(8,128)(2,1)S(1)} %arrange.1.refs_2_, bf16[1792,1024]{1,0:T(8,128)(2,1)S(1)} %down.6.refs_3_), custom_call_target="tpu_custom_call" | custom-call | tf_op jit(solution)/shard_map/down/pallas_call | solution.py:365
  (74 shorter events, 23.6 us)
Async XLA Ops:
  11.7 12.8 %collective-permute-start.1 = (bf16[256,1024]{1,0:T(8,128)(2,1)S(1)}, bf16[256,1024]{1,0:T(8,128)(2,1)S(1)}, u32[]{:S(2)}, u32[]{:S(2)}) collective-permute-start(bf16[256,1024]{1,0:T(8,128)(2,1)S(1)} %get-tuple-element.34), channel_id=1, source_target_pairs={{0,2},{1,3},{2,0},{3,1},{4,6},{5,7},{6,4},{7,5},{8,10},{9,11},{10,... | collective-permute-start | bytes 1572872 | tf_op jit(solution)/shard_map/ppermute | solution.py:30
  19.1 6.6 %collective-permute-start.4 = (bf16[256,768]{1,0:T(8,128)(2,1)S(1)}, bf16[256,768]{1,0:T(8,128)(2,1)S(1)}, u32[]{:S(2)}, u32[]{:S(2)}) collective-permute-start(bf16[256,768]{1,0:T(8,128)(2,1)S(1)} %get-tuple-element.40), channel_id=1, source_target_pairs={{0,2},{1,3},{2,0},{3,1},{4,6},{5,7},{6,4},{7,5},{8,10},{9,11},{10,... | collective-permute-start | bytes 1179656 | tf_op jit(solution)/shard_map/ppermute | solution.py:30
  20.0 56.1 %collective-permute-start.19 = (bf16[1792,256]{1,0:T(8,128)(2,1)S(1)}, bf16[1792,256]{1,0:T(8,128)(2,1)}, u32[]{:S(2)}, u32[]{:S(2)}) collective-permute-start(bf16[1792,256]{1,0:T(8,128)(2,1)S(1)} %dequant.1.refs_0_), channel_id=1, source_target_pairs={{0,5},{1,4},{2,7},{3,6},{4,1},{5,0},{6,3},{7,2},{8,13},{9,12},{10,... | collective-permute-start | bytes 2752520 | tf_op jit(solution)/shard_map/ppermute | solution.py:30
  24.5 51.9 %collective-permute-start.18 = (bf16[1792,256]{1,0:T(8,128)(2,1)S(1)}, bf16[1792,256]{1,0:T(8,128)(2,1)}, u32[]{:S(2)}, u32[]{:S(2)}) collective-permute-start(bf16[1792,256]{1,0:T(8,128)(2,1)S(1)} %dequant.1.refs_0_), channel_id=1, source_target_pairs={{0,4},{1,5},{2,6},{3,7},{4,0},{5,1},{6,2},{7,3},{8,12},{9,13},{10,... | collective-permute-start | bytes 2752520 | tf_op jit(solution)/shard_map/ppermute | solution.py:30
  25.7 41.7 %collective-permute-start.2 = (bf16[256,1024]{1,0:T(8,128)(2,1)}, bf16[256,1024]{1,0:T(8,128)(2,1)}, u32[]{:S(2)}, u32[]{:S(2)}) collective-permute-start(bf16[256,1024]{1,0:T(8,128)(2,1)} %shard_map.85), channel_id=1, source_target_pairs={{0,4},{1,5},{2,6},{3,7},{4,0},{5,1},{6,2},{7,3},{8,12},{9,13},{10,... | collective-permute-start | bytes 1572872 | tf_op jit(solution)/shard_map/ppermute | solution.py:30
  29.1 38.4 %collective-permute-start.5 = (bf16[256,768]{1,0:T(8,128)(2,1)}, bf16[256,768]{1,0:T(8,128)(2,1)}, u32[]{:S(2)}, u32[]{:S(2)}) collective-permute-start(bf16[256,768]{1,0:T(8,128)(2,1)} %shard_map.86), channel_id=1, source_target_pairs={{0,4},{1,5},{2,6},{3,7},{4,0},{5,1},{6,2},{7,3},{8,12},{9,13},{10,... | collective-permute-start | bytes 1179656 | tf_op jit(solution)/shard_map/ppermute | solution.py:30
  30.4 55.2 %collective-permute-start.22 = (bf16[256,1024]{1,0:T(8,128)(2,1)S(1)}, bf16[256,1024]{1,0:T(8,128)(2,1)S(1)}, u32[]{:S(2)}, u32[]{:S(2)}) collective-permute-start(bf16[256,1024]{1,0:T(8,128)(2,1)S(1)} %shard_map.91), channel_id=1, source_target_pairs={{0,1},{1,0},{2,3},{3,2},{4,5},{5,4},{6,7},{7,6},{8,9},{9,8},{10,11... | collective-permute-start | bytes 1572872 | tf_op jit(solution)/shard_map/ppermute | solution.py:30
  71.5 6.9 %collective-permute-start.6 = (bf16[64,1792]{1,0:T(8,128)(2,1)S(1)}, bf16[64,1792]{1,0:T(8,128)(2,1)S(1)}, u32[]{:S(2)}, u32[]{:S(2)}) collective-permute-start(bf16[64,1792]{1,0:T(8,128)(2,1)S(1)} %get-tuple-element.42), channel_id=1, source_target_pairs={{0,8},{1,9},{2,34},{3,35},{4,12},{5,13},{6,38},{7,39},{8,0},{9,1},... | collective-permute-start | bytes 688136 | tf_op jit(solution)/shard_map/ppermute | solution.py:30
  73.2 9.5 %collective-permute-start.7 = (bf16[64,1792]{1,0:T(8,128)(2,1)S(1)}, bf16[64,1792]{1,0:T(8,128)(2,1)S(1)}, u32[]{:S(2)}, u32[]{:S(2)}) collective-permute-start(bf16[64,1792]{1,0:T(8,128)(2,1)S(1)} %get-tuple-element.43), channel_id=1, source_target_pairs={{0,16},{1,17},{2,66},{3,67},{4,20},{5,21},{6,70},{7,71},{8,24},{9,... | collective-permute-start | bytes 688136 | tf_op jit(solution)/shard_map/ppermute | solution.py:30
  76.1 8.9 %collective-permute-start.8 = (bf16[64,1792]{1,0:T(8,128)(2,1)S(1)}, bf16[64,1792]{1,0:T(8,128)(2,1)S(1)}, u32[]{:S(2)}, u32[]{:S(2)}) collective-permute-start(bf16[64,1792]{1,0:T(8,128)(2,1)S(1)} %get-tuple-element.44), channel_id=1, source_target_pairs={{0,24},{1,25},{2,98},{3,99},{4,28},{5,29},{6,102},{7,103},{8,16},{... | collective-permute-start | bytes 688136 | tf_op jit(solution)/shard_map/ppermute | solution.py:30
  78.0 36.3 %collective-permute-start.20 = (bf16[1792,256]{1,0:T(8,128)(2,1)S(1)}, bf16[1792,256]{1,0:T(8,128)(2,1)S(1)}, u32[]{:S(2)}, u32[]{:S(2)}) collective-permute-start(bf16[1792,256]{1,0:T(8,128)(2,1)S(1)} %shard_map.90), channel_id=1, source_target_pairs={{0,5},{1,4},{2,6},{3,7},{4,1},{5,0},{6,2},{7,3},{8,13},{9,12},{10,... | collective-permute-start | bytes 2752520 | tf_op jit(solution)/shard_map/ppermute | solution.py:30
  85.4 7.7 %collective-permute-start.10 = (bf16[64,1792]{1,0:T(8,128)(2,1)S(1)}, bf16[64,1792]{1,0:T(8,128)(2,1)S(1)}, u32[]{:S(2)}, u32[]{:S(2)}) collective-permute-start(bf16[64,1792]{1,0:T(8,128)(2,1)S(1)} %get-tuple-element.47), channel_id=1, source_target_pairs={{0,16},{1,17},{2,66},{3,67},{4,20},{5,21},{6,70},{7,71},{8,24},{9,... | collective-permute-start | bytes 688136 | tf_op jit(solution)/shard_map/ppermute | solution.py:30
  85.6 19.7 %collective-permute-start.23 = (bf16[256,1024]{1,0:T(8,128)(2,1)S(1)}, bf16[256,1024]{1,0:T(8,128)(2,1)S(1)}, u32[]{:S(2)}, u32[]{:S(2)}) collective-permute-start(bf16[256,1024]{1,0:T(8,128)(2,1)S(1)} %collective-permute-done.22.a_ref.g0), channel_id=1, source_target_pairs={{0,24},{1,25},{2,98},{3,99},{4,28},{5,29},{6,102},{7,103},{8,16},{... | collective-permute-start | bytes 1572872 | tf_op jit(solution)/shard_map/ppermute | solution.py:30
  87.8 27.3 %collective-permute-start.27 = (bf16[1792,256]{1,0:T(8,128)(2,1)S(1)}, bf16[1792,256]{1,0:T(8,128)(2,1)S(1)}, u32[]{:S(2)}, u32[]{:S(2)}) collective-permute-start(bf16[1792,256]{1,0:T(8,128)(2,1)S(1)} %dequant.1.refs_0_), channel_id=1, source_target_pairs={{0,2},{1,3},{2,0},{3,1},{4,6},{5,7},{6,4},{7,5},{8,10},{9,11},{10,... | collective-permute-start | bytes 2752520 | tf_op jit(solution)/shard_map/ppermute | solution.py:30
  87.8 13.1 %collective-permute-start.11 = (bf16[64,1792]{1,0:T(8,128)(2,1)S(1)}, bf16[64,1792]{1,0:T(8,128)(2,1)S(1)}, u32[]{:S(2)}, u32[]{:S(2)}) collective-permute-start(bf16[64,1792]{1,0:T(8,128)(2,1)S(1)} %get-tuple-element.48), channel_id=1, source_target_pairs={{0,24},{1,25},{2,98},{3,99},{4,28},{5,29},{6,102},{7,103},{8,16},{... | collective-permute-start | bytes 688136 | tf_op jit(solution)/shard_map/ppermute | solution.py:30
  93.1 7.9 %collective-permute-start.9 = (bf16[64,1792]{1,0:T(8,128)(2,1)S(1)}, bf16[64,1792]{1,0:T(8,128)(2,1)S(1)}, u32[]{:S(2)}, u32[]{:S(2)}) collective-permute-start(bf16[64,1792]{1,0:T(8,128)(2,1)S(1)} %get-tuple-element.46), channel_id=1, source_target_pairs={{0,8},{1,9},{2,34},{3,35},{4,12},{5,13},{6,38},{7,39},{8,0},{9,1},... | collective-permute-start | bytes 688136 | tf_op jit(solution)/shard_map/ppermute | solution.py:30
  102.6 9.3 %collective-permute-start.13 = (bf16[64,1792]{1,0:T(8,128)(2,1)S(1)}, bf16[64,1792]{1,0:T(8,128)(2,1)S(1)}, u32[]{:S(2)}, u32[]{:S(2)}) collective-permute-start(bf16[64,1792]{1,0:T(8,128)(2,1)S(1)} %get-tuple-element.51), channel_id=1, source_target_pairs={{0,64},{1,65},{2,18},{3,19},{4,68},{5,69},{6,22},{7,23},{8,72},{9,... | collective-permute-start | bytes 688136 | tf_op jit(solution)/shard_map/ppermute | solution.py:30
  105.4 8.9 %collective-permute-start.14 = (bf16[64,1792]{1,0:T(8,128)(2,1)S(1)}, bf16[64,1792]{1,0:T(8,128)(2,1)S(1)}, u32[]{:S(2)}, u32[]{:S(2)}) collective-permute-start(bf16[64,1792]{1,0:T(8,128)(2,1)S(1)} %get-tuple-element.52), channel_id=1, source_target_pairs={{0,96},{1,97},{2,26},{3,27},{4,100},{5,101},{6,30},{7,31},{8,104},... | collective-permute-start | bytes 688136 | tf_op jit(solution)/shard_map/ppermute | solution.py:30
  107.2 31.1 %collective-permute-start.24 = (bf16[2,256,1024]{2,1,0:T(8,128)(2,1)S(1)}, bf16[2,256,1024]{2,1,0:T(8,128)(2,1)S(1)}, u32[]{:S(2)}, u32[]{:S(2)}) collective-permute-start(bf16[2,256,1024]{2,1,0:T(8,128)(2,1)S(1)} %shard_map.92), channel_id=1, source_target_pairs={{0,96},{1,97},{2,26},{3,27},{4,100},{5,101},{6,30},{7,31},{8,104},... | collective-permute-start | bytes 3145736 | tf_op jit(solution)/shard_map/ppermute | solution.py:30
  111.9 26.6 %collective-permute-start.26 = (bf16[1792,256]{1,0:T(8,128)(2,1)}, bf16[1792,256]{1,0:T(8,128)(2,1)S(1)}, u32[]{:S(2)}, u32[]{:S(2)}) collective-permute-start(bf16[1792,256]{1,0:T(8,128)(2,1)} %collective-permute-done.19.b_ref.refs_0_), channel_id=1, source_target_pairs={{0,2},{1,3},{2,0},{3,1},{4,6},{5,7},{6,4},{7,5},{8,10},{9,11},{10,... | collective-permute-start | bytes 2752520 | tf_op jit(solution)/shard_map/ppermute | solution.py:30
  114.3 27.5 %collective-permute-start.25 = (bf16[1792,256]{1,0:T(8,128)(2,1)}, bf16[1792,256]{1,0:T(8,128)(2,1)S(1)}, u32[]{:S(2)}, u32[]{:S(2)}) collective-permute-start(bf16[1792,256]{1,0:T(8,128)(2,1)} %collective-permute-done.18.a_ref.refs_0_), channel_id=1, source_target_pairs={{0,2},{1,3},{2,0},{3,1},{4,6},{5,7},{6,4},{7,5},{8,10},{9,11},{10,... | collective-permute-start | bytes 2752520 | tf_op jit(solution)/shard_map/ppermute | solution.py:30
  114.3 30.8 %collective-permute-start.21 = (bf16[1792,256]{1,0:T(8,128)(2,1)S(1)}, bf16[1792,256]{1,0:T(8,128)(2,1)S(1)}, u32[]{:S(2)}, u32[]{:S(2)}) collective-permute-start(bf16[1792,256]{1,0:T(8,128)(2,1)S(1)} %collective-permute-done.20.refs_0_), channel_id=1, source_target_pairs={{0,2},{1,3},{2,0},{3,1},{4,6},{5,7},{6,4},{7,5},{8,10},{9,11},{10,... | collective-permute-start | bytes 2752520 | tf_op jit(solution)/shard_map/ppermute | solution.py:30
  121.4 7.5 %collective-permute-start.16 = (bf16[64,1792]{1,0:T(8,128)(2,1)S(1)}, bf16[64,1792]{1,0:T(8,128)(2,1)S(1)}, u32[]{:S(2)}, u32[]{:S(2)}) collective-permute-start(bf16[64,1792]{1,0:T(8,128)(2,1)S(1)} %get-tuple-element.55), channel_id=1, source_target_pairs={{0,64},{1,65},{2,18},{3,19},{4,68},{5,69},{6,22},{7,23},{8,72},{9,... | collective-permute-start | bytes 688136 | tf_op jit(solution)/shard_map/ppermute | solution.py:30
  129.0 7.2 %collective-permute-start.17 = (bf16[64,1792]{1,0:T(8,128)(2,1)S(1)}, bf16[64,1792]{1,0:T(8,128)(2,1)S(1)}, u32[]{:S(2)}, u32[]{:S(2)}) collective-permute-start(bf16[64,1792]{1,0:T(8,128)(2,1)S(1)} %get-tuple-element.56), channel_id=1, source_target_pairs={{0,96},{1,97},{2,26},{3,27},{4,100},{5,101},{6,30},{7,31},{8,104},... | collective-permute-start | bytes 688136 | tf_op jit(solution)/shard_map/ppermute | solution.py:30
  (16 other events, 122.9 us)

commit v3 on v2

--- a/solution.py
+++ b/solution.py
@@ -106,11 +106,11 @@
     weights(0).start()
     for copy in rows:
         copy.start()
+    for copy in rows:
+        copy.wait()
     for tile in range(1, count // TILE):
         weights(tile).start()
     rest.start()
-    for copy in rows:
-        copy.wait()
 
     def body(tile, carry):
         weights(tile).wait()
@@ -135,7 +135,7 @@
         out_specs=[VMEM_SPEC] * 6,
         scratch_shapes=[pltpu.VMEM((count, width), BF16), pltpu.VMEM((total, TILE), BF16), pltpu.SemaphoreType.DMA((4,)),
                         pltpu.SemaphoreType.DMA((count // TILE,)), pltpu.SemaphoreType.DMA(())],
-        compiler_params=pltpu.CompilerParams(vmem_limit_bytes=52 << 20),
+        compiler_params=pltpu.CompilerParams(vmem_limit_bytes=49 << 20),
         name="first_product",
     )(rows, weight)
 
@@ -205,9 +205,8 @@
             out_ref[...] = source[...]
 
 
-def rotate_kernel(*refs, scale, parts):
-    codes_ref = refs[3 * len(parts)]
-    outs, mixed_ref = refs[3 * len(parts) + 1:-1], refs[-1]
+def rotate_kernel(keep_ref, away_ref, far_ref, codes_ref, *refs, scale, start):
+    outs, mixed_ref = refs[:-1], refs[-1]
     rows = outs[0].shape[0]
     mine = place(0)
     row = lax.broadcasted_iota(jnp.int32, (TILE, TILE), 0)
@@ -217,31 +216,28 @@
         bits = bits ^ (bits >> shift)
     sign = (1 - 2 * (bits & 1)).astype(F32)
     table = jnp.where((row ^ col) < BLOCK, sign, 0.0).astype(BF16)
-    for part, (start, count) in enumerate(parts):
-        keep_ref, away_ref, far_ref = refs[3 * part:3 * part + 3]
-        for first in range(0, count, TILE):
-            here = pl.ds(first, TILE)
-            cols = pl.ds(start + first, TILE)
-            total = keep_ref[:, here].astype(F32) + away_ref[:, here].astype(F32) + far_ref[:, here].astype(F32)
-            codes = codes_ref[:, cols]
-            masked = jnp.where((codes > -128) & (codes < 127), total, 0.0).astype(BF16)
-            mixed = jnp.dot(masked, table, preferred_element_type=F32)
-            mixed_ref[:, cols] = (mixed * scale).astype(BF16)
+    for first in range(0, far_ref.shape[1], TILE):
+        cols = pl.ds(first, TILE)
+        total = keep_ref[:, cols].astype(F32) + away_ref[:, cols].astype(F32) + far_ref[:, cols].astype(F32)
+        codes = codes_ref[:, pl.ds(start + first, TILE)]
+        masked = jnp.where((codes > -128) & (codes < 127), total, 0.0).astype(BF16)
+        mixed = jnp.dot(masked, table, preferred_element_type=F32)
+        mixed_ref[:, cols] = (mixed * scale).astype(BF16)
     for step, out in enumerate(outs):
         out[...] = mixed_ref[pl.ds(pl.multiple_of((mine ^ step) * rows, rows), rows), :]
 
 
-def rotate(sums, codes, scale):
-    tokens, hidden = codes.shape
-    return pl.pallas_call(
-        functools.partial(rotate_kernel, scale=scale, parts=PARTS),
-        out_shape=[pltpu.VMEM((tokens // 4, hidden), BF16)] * 4,
-        in_specs=[VMEM_SPEC] * (3 * len(PARTS) + 1),
+def rotate(sums, codes, start, scale):
+    tokens, count = sums[0].shape
+    return pl.pallas_call(
+        functools.partial(rotate_kernel, scale=scale, start=start),
+        out_shape=[pltpu.VMEM((tokens // 4, count), BF16)] * 4,
+        in_specs=[VMEM_SPEC] * 4,
         out_specs=[VMEM_SPEC] * 4,
-        scratch_shapes=[pltpu.VMEM((tokens, hidden), BF16)],
+        scratch_shapes=[pltpu.VMEM((tokens, count), BF16)],
         compiler_params=SMALL,
         name="rotate",
-    )(*[value for group in sums for value in group], codes)
+    )(*sums, codes)
 
 
 def parity(value):
@@ -249,17 +245,20 @@
 
 
 def mix_kernel(*refs, axis):
+    groups, outs = [refs[i:i + 4] for i in range(0, len(refs) - 4, 4)], refs[-4:]
     mine = place(axis)
     signs = [parity(mine & step) for step in range(4)]
     whole = parity(mine)
-    hidden = refs[0].shape[1]
-    for first in range(0, hidden, TILE):
-        cols = pl.ds(first, TILE)
-        p0, p1, p2, p3 = [refs[step][:, cols].astype(F32) * signs[step] for step in range(4)]
-        even, odd = (p0 + p1, p2 + p3), (p0 - p1, p2 - p3)
-        outs = (even[0] + even[1], odd[0] + odd[1], even[0] - even[1], odd[0] - odd[1])
-        for step in range(4):
-            refs[4 + step][:, cols] = (outs[step] * (whole * signs[step])).astype(BF16)
+    start = 0
+    for group in groups:
+        for first in range(0, group[0].shape[1], TILE):
+            here, cols = pl.ds(first, TILE), pl.ds(start + first, TILE)
+            p0, p1, p2, p3 = [group[step][:, here].astype(F32) * signs[step] for step in range(4)]
+            even, odd = (p0 + p1, p2 + p3), (p0 - p1, p2 - p3)
+            mixed = (even[0] + even[1], odd[0] + odd[1], even[0] - even[1], odd[0] - odd[1])
+            for step in range(4):
+                outs[step][:, cols] = (mixed[step] * (whole * signs[step])).astype(BF16)
+        start += group[0].shape[1]
 
 
 def relabel_kernel(*refs):
@@ -272,18 +271,21 @@
 
 
 def four(kernel, pieces):
+    rows = pieces[0].shape[0]
+    width = sum(piece.shape[1] for piece in pieces[::4])
     return pl.pallas_call(
         kernel,
-        out_shape=[pltpu.VMEM(pieces[0].shape, BF16)] * 4,
-        in_specs=[VMEM_SPEC] * 4,
+        out_shape=[pltpu.VMEM((rows, width), BF16)] * 4,
+        in_specs=[VMEM_SPEC] * len(pieces),
         out_specs=[VMEM_SPEC] * 4,
         compiler_params=SMALL,
     )(*pieces)
 
 
-def finish_kernel(p0, p1, p2, p3, gate_ref, up_ref, gate_out, up_out):
+def finish_kernel(p0, p1, p2, p3, gate_ref, up_ref, gate_out, up_out, gate_buf, up_buf, sem):
     mine = place(1)
     rows = p0.shape[0]
+    copies = []
     for step, piece in enumerate((p0, p1, p2, p3)):
         span = pl.ds(pl.multiple_of((mine ^ step) * rows, rows), rows)
         for first in range(0, piece.shape[1], TILE):
@@ -292,16 +294,24 @@
             gate = gate_ref[span, cols].astype(F32)
             up = up_ref[span, cols].astype(F32)
             sig = jax.nn.sigmoid(gate)
-            gate_out[span, cols] = (hidden * up * sig * (1.0 + gate * (1.0 - sig))).astype(BF16)
-            up_out[span, cols] = (hidden * gate * sig).astype(BF16)
+            gate_buf[step, :, cols] = (hidden * up * sig * (1.0 + gate * (1.0 - sig))).astype(BF16)
+            up_buf[step, :, cols] = (hidden * gate * sig).astype(BF16)
+        copies.append(pltpu.make_async_copy(gate_buf.at[step], gate_out.at[span], sem.at[2 * step]))
+        copies.append(pltpu.make_async_copy(up_buf.at[step], up_out.at[span], sem.at[2 * step + 1]))
+        copies[-2].start()
+        copies[-1].start()
+    for copy in copies:
+        copy.wait()
 
 
 def finish(pieces, gate, up):
+    shape = (4, *pieces[0].shape)
     return pl.pallas_call(
         finish_kernel,
         out_shape=[jax.ShapeDtypeStruct(gate.shape, BF16)] * 2,
         in_specs=[VMEM_SPEC] * 6,
-        out_specs=[VMEM_SPEC] * 2,
+        out_specs=[ANY_SPEC] * 2,
+        scratch_shapes=[pltpu.VMEM(shape, BF16), pltpu.VMEM(shape, BF16), pltpu.SemaphoreType.DMA((8,))],
         compiler_params=SMALL,
         name="finish",
     )(*pieces, gate, up)
@@ -421,8 +431,10 @@
             moved[step] = send(pieces[step], along(axis, step))
         return moved
 
-    pieces = rotate(sums, codes, scale)
-    pieces = spread(pieces, 0)
+    pieces = []
+    for part, (first, count) in enumerate(PARTS):
+        turned = rotate(sums[part], codes, first, scale)
+        pieces += spread(turned, 0)
     pieces = four(functools.partial(mix_kernel, axis=0), pieces)
     pieces = spread(pieces, 0)
     pieces = four(relabel_kernel, pieces)

time: 150 us -> 141 us (0.940)
  waiting for transfers between devices: 77.5 us -> 64.4 us
  starting transfers between devices: 26.4 us -> 35.7 us
  local copies, waits for them, and re-layouts: 7.83 us -> 3.83 us
    ppermute x28 -> x31, waiting for transfers between devices: 77.5 us -> 64.4 us  [send(): return lax.ppermute(value, AXES, route)]
    ppermute x28 -> x31, starting transfers between devices: 26.4 us -> 35.7 us  [send(): return lax.ppermute(value, AXES, route)]
    unnamed x24, local copies, waits for them, and re-layouts: 7.83 us -> 3.83 us
    pallas_call x4 -> x5, Pallas kernels: 2.88 us -> 3.9 us  [the longest x2 3.11 us: rotate(): pl.pallas_call(functools.partial(rotate_kernel, scale=scale, start=start)...]
  transfers between devices with their start and end apart: 28 -> 31, of which waited for: 11 -> 12; matrix products, arithmetic and copies ran while one was open for 0% -> 0% of each run, Pallas kernels for 15% -> 16%
where the time goes in v3:
time: 141 us
  waiting for transfers between devices  64.4 us (46%)
  Pallas kernels  36.1 us (26%)
  starting transfers between devices  35.7 us (25%)
  local copies, waits for them, and re-layouts  3.83 us (3%)
    ppermute x31, waiting for transfers between devices, send(): return lax.ppermute(value, AXES, route)  64.4 us
    ppermute x31, starting transfers between devices, send(): return lax.ppermute(value, AXES, route)  35.7 us
    pallas_call x4, Pallas kernels, down(): pl.pallas_call(functools.partial(down_kernel, flips=flips, summed=acc is...  12.9 us
    pallas_call x1, Pallas kernels, first_product(): pl.pallas_call(first_product_kernel, out_shape=[pltpu.VMEM((total // 4, c...  8.8 us
    pallas_call x1, Pallas kernels, second_product(): pl.pallas_call(second_product_kernel, out_shape=[pltpu.VMEM((total // 4,...  3.99 us
    pallas_call x5, Pallas kernels, small(): pl.pallas_call(kernel, out_shape=pltpu.VMEM(shape, BF16), in_specs=[spec...  3.83 us
    unnamed x24, local copies, waits for them, and re-layouts  3.83 us
    pallas_call x2, Pallas kernels, rotate(): pl.pallas_call(functools.partial(rotate_kernel, scale=scale, start=start)...  3.11 us
  transfers between devices with their start and end apart: 31, of which 12 were waited for; matrix products, arithmetic and copies ran while one was open for 0% of the time, Pallas kernels for 16%

profile of v3, /device:TPU:0, one launch (start us, length us, event | category | flops | bytes accessed | tf_op | source)
XLA Modules:
  0.0 141.1 jit_solution(18333750378146408627)
XLA Ops:
  0.6 8.8 %first_product.1 = (bf16[256,1024]{1,0:T(8,128)(2,1)S(1)}, bf16[256,1024]{1,0:T(8,128)(2,1)S(1)}, bf16[256,1024]{1,0:T(8,128)(2,1)}, bf16[256,1024]{1,0:T(8,128)...) custom-call(bf16[1024,2048]{1,0:T(8,128)(2,1)} %bitcast.13, bf16[1792,2048]{1,0:T(8,128)(2,1)} %w_ref.1), custom_call_target="tpu_custom_call" | custom-call | tf_op jit(solution)/shard_map/first_product/pallas_call | solution.py:130
  9.6 4.0 %second_product.1 = (bf16[256,768]{1,0:T(8,128)(2,1)S(1)}, bf16[256,768]{1,0:T(8,128)(2,1)S(1)}, bf16[256,768]{1,0:T(8,128)(2,1)S(1)}, bf16[256,768]{1,0:T(8,128)(2,1)S(1)}) custom-call(bf16[1024,2048]{1,0:T(8,128)(2,1)S(1)} %get-tuple-element.43.rows_ref.refs_2_, bf16[768,2048]{1,0:T(8,128)(2,1)S(1)} %get-tuple-element.44.w_ref), custom_call_target="tpu_custom_call" | custom-call | tf_op jit(solution)/shard_map/second_product/pallas_call | solution.py:158
  15.0 4.3 %collective-permute-start.22 = (bf16[1792,256]{1,0:T(8,128)(2,1)S(1)}, bf16[1792,256]{1,0:T(8,128)(2,1)}, u32[]{:S(2)}, u32[]{:S(2)}) collective-permute-start(bf16[1792,256]{1,0:T(8,128)(2,1)S(1)} %dequant.1.refs_0_), channel_id=1, source_target_pairs={{0,5},{1,4},{2,7},{3,6},{4,1},{5,0},{6,3},{7,2},{8,13},{9,12},{10,... | collective-permute-start | bytes 2752520 | tf_op jit(solution)/shard_map/ppermute | solution.py:30
  24.4 26.7 %collective-permute-done.8.far_ref = bf16[256,768]{1,0:T(8,128)(2,1)} collective-permute-done((bf16[256,768]{1,0:T(8,128)(2,1)}, bf16[256,768]{1,0:T(8,128)(2,1)}, u32[]{:S(2)}, u32[]{:S(2)}) %collective-permute-start.8) | collective-permute-done | bytes 393248 | tf_op jit(solution)/shard_map/ppermute | solution.py:30
  54.6 3.3 %collective-permute-start.10 = (bf16[64,768]{1,0:T(8,128)(2,1)S(1)}, bf16[64,768]{1,0:T(8,128)(2,1)S(1)}, u32[]{:S(2)}, u32[]{:S(2)}) collective-permute-start(bf16[64,768]{1,0:T(8,128)(2,1)S(1)} %get-tuple-element.51), channel_id=1, source_target_pairs={{0,16},{1,17},{2,66},{3,67},{4,20},{5,21},{6,70},{7,71},{8,24},{9,... | collective-permute-start | bytes 294920 | tf_op jit(solution)/shard_map/ppermute | solution.py:30
  57.8 2.9 %collective-permute-done.10.refs_6_ = bf16[64,768]{1,0:T(8,128)(2,1)S(1)} collective-permute-done((bf16[64,768]{1,0:T(8,128)(2,1)S(1)}, bf16[64,768]{1,0:T(8,128)(2,1)S(1)}, u32[]{:S(2)}, u32[]{:S(2)}) %collective-permute-start.10) | collective-permute-done | bytes 98336 | tf_op jit(solution)/shard_map/ppermute | solution.py:30
  60.8 3.0 %collective-permute-start.11 = (bf16[64,768]{1,0:T(8,128)(2,1)S(1)}, bf16[64,768]{1,0:T(8,128)(2,1)S(1)}, u32[]{:S(2)}, u32[]{:S(2)}) collective-permute-start(bf16[64,768]{1,0:T(8,128)(2,1)S(1)} %get-tuple-element.52), channel_id=1, source_target_pairs={{0,24},{1,25},{2,98},{3,99},{4,28},{5,29},{6,102},{7,103},{8,16},{... | collective-permute-start | bytes 294920 | tf_op jit(solution)/shard_map/ppermute | solution.py:30
  66.7 1.9 %collective-permute-start.3 = (bf16[64,1024]{1,0:T(8,128)(2,1)S(1)}, bf16[64,1024]{1,0:T(8,128)(2,1)S(1)}, u32[]{:S(2)}, u32[]{:S(2)}) collective-permute-start(bf16[64,1024]{1,0:T(8,128)(2,1)S(1)} %get-tuple-element.40), channel_id=1, source_target_pairs={{0,8},{1,9},{2,34},{3,35},{4,12},{5,13},{6,38},{7,39},{8,0},{9,1},... | collective-permute-start | bytes 393224 | tf_op jit(solution)/shard_map/ppermute | solution.py:30
  68.6 2.4 %collective-permute-start.4 = (bf16[64,1024]{1,0:T(8,128)(2,1)S(1)}, bf16[64,1024]{1,0:T(8,128)(2,1)S(1)}, u32[]{:S(2)}, u32[]{:S(2)}) collective-permute-start(bf16[64,1024]{1,0:T(8,128)(2,1)S(1)} %get-tuple-element.41), channel_id=1, source_target_pairs={{0,16},{1,17},{2,66},{3,67},{4,20},{5,21},{6,70},{7,71},{8,24},{9,... | collective-permute-start | bytes 393224 | tf_op jit(solution)/shard_map/ppermute | solution.py:30
  73.2 2.7 %collective-permute-start.23 = (bf16[1792,256]{1,0:T(8,128)(2,1)S(1)}, bf16[1792,256]{1,0:T(8,128)(2,1)S(1)}, u32[]{:S(2)}, u32[]{:S(2)}) collective-permute-start(bf16[1792,256]{1,0:T(8,128)(2,1)S(1)} %shard_map.90), channel_id=1, source_target_pairs={{0,5},{1,4},{2,6},{3,7},{4,1},{5,0},{6,2},{7,3},{8,13},{9,12},{10,... | collective-permute-start | bytes 2752520 | tf_op jit(solution)/shard_map/ppermute | solution.py:30
  79.6 2.2 %collective-permute-start.13 = (bf16[64,1792]{1,0:T(8,128)(2,1)S(1)}, bf16[64,1792]{1,0:T(8,128)(2,1)S(1)}, u32[]{:S(2)}, u32[]{:S(2)}) collective-permute-start(bf16[64,1792]{1,0:T(8,128)(2,1)S(1)} %get-tuple-element.55), channel_id=1, source_target_pairs={{0,16},{1,17},{2,66},{3,67},{4,20},{5,21},{6,70},{7,71},{8,24},{9,... | collective-permute-start | bytes 688136 | tf_op jit(solution)/shard_map/ppermute | solution.py:30
  85.1 2.1 %collective-permute-done.13.refs_2_ = bf16[64,1792]{1,0:T(8,128)(2,1)S(1)} collective-permute-done((bf16[64,1792]{1,0:T(8,128)(2,1)S(1)}, bf16[64,1792]{1,0:T(8,128)(2,1)S(1)}, u32[]{:S(2)}, u32[]{:S(2)}) %collective-permute-start.13) | collective-permute-done | bytes 229408 | tf_op jit(solution)/shard_map/ppermute | solution.py:30
  87.2 5.9 %collective-permute-done.14.refs_3_ = bf16[64,1792]{1,0:T(8,128)(2,1)S(1)} collective-permute-done((bf16[64,1792]{1,0:T(8,128)(2,1)S(1)}, bf16[64,1792]{1,0:T(8,128)(2,1)S(1)}, u32[]{:S(2)}, u32[]{:S(2)}) %collective-permute-start.14) | collective-permute-done | bytes 229408 | tf_op jit(solution)/shard_map/ppermute | solution.py:30
  94.8 2.7 %collective-permute-start.16 = (bf16[64,1792]{1,0:T(8,128)(2,1)S(1)}, bf16[64,1792]{1,0:T(8,128)(2,1)S(1)}, u32[]{:S(2)}, u32[]{:S(2)}) collective-permute-start(bf16[64,1792]{1,0:T(8,128)(2,1)S(1)} %get-tuple-element.59), channel_id=1, source_target_pairs={{0,64},{1,65},{2,18},{3,19},{4,68},{5,69},{6,22},{7,23},{8,72},{9,... | collective-permute-start | bytes 688136 | tf_op jit(solution)/shard_map/ppermute | solution.py:30
  99.3 2.7 %collective-permute-start.27 = (bf16[2,256,1024]{2,1,0:T(8,128)(2,1)S(1)}, bf16[2,256,1024]{2,1,0:T(8,128)(2,1)S(1)}, u32[]{:S(2)}, u32[]{:S(2)}) collective-permute-start(bf16[2,256,1024]{2,1,0:T(8,128)(2,1)S(1)} %shard_map.92), channel_id=1, source_target_pairs={{0,96},{1,97},{2,26},{3,27},{4,100},{5,101},{6,30},{7,31},{8,104},... | collective-permute-start | bytes 3145736 | tf_op jit(solution)/shard_map/ppermute | solution.py:30
  102.0 2.0 %collective-permute-done.16.refs_2_ = bf16[64,1792]{1,0:T(8,128)(2,1)S(1)} collective-permute-done((bf16[64,1792]{1,0:T(8,128)(2,1)S(1)}, bf16[64,1792]{1,0:T(8,128)(2,1)S(1)}, u32[]{:S(2)}, u32[]{:S(2)}) %collective-permute-start.16) | collective-permute-done | bytes 229408 | tf_op jit(solution)/shard_map/ppermute | solution.py:30
  104.0 2.4 %collective-permute-done.17.refs_3_ = bf16[64,1792]{1,0:T(8,128)(2,1)S(1)} collective-permute-done((bf16[64,1792]{1,0:T(8,128)(2,1)S(1)}, bf16[64,1792]{1,0:T(8,128)(2,1)S(1)}, u32[]{:S(2)}, u32[]{:S(2)}) %collective-permute-start.17) | collective-permute-done | bytes 229408 | tf_op jit(solution)/shard_map/ppermute | solution.py:30
  107.4 6.0 %collective-permute-done.18.p1 = bf16[64,1792]{1,0:T(8,128)(2,1)S(1)} collective-permute-done((bf16[64,1792]{1,0:T(8,128)(2,1)S(1)}, bf16[64,1792]{1,0:T(8,128)(2,1)S(1)}, u32[]{:S(2)}, u32[]{:S(2)}) %collective-permute-start.18) | collective-permute-done | bytes 229408 | tf_op jit(solution)/shard_map/ppermute | solution.py:30
  113.8 7.1 %collective-permute-done.19.p2 = bf16[64,1792]{1,0:T(8,128)(2,1)S(1)} collective-permute-done((bf16[64,1792]{1,0:T(8,128)(2,1)S(1)}, bf16[64,1792]{1,0:T(8,128)(2,1)S(1)}, u32[]{:S(2)}, u32[]{:S(2)}) %collective-permute-start.19) | collective-permute-done | bytes 229408 | tf_op jit(solution)/shard_map/ppermute | solution.py:30
  121.4 2.1 %down.4.refs_3_ = bf16[1792,1024]{1,0:T(8,128)(2,1)S(1)} custom-call(bf16[1792,256]{1,0:T(8,128)(2,1)S(1)} %dequant.1.refs_0_, bf16[1792,256]{1,0:T(8,128)(2,1)S(1)} %collective-permute-done.30.refs_1_, bf16[1024,2048]{1,0:T(8,128)(2,1)S(1)} %copy-done.1), custom_call_target="tpu_custom_call" | custom-call | tf_op jit(solution)/shard_map/down/pallas_call | solution.py:375
  123.5 4.6 %collective-permute-done.20.p3 = bf16[64,1792]{1,0:T(8,128)(2,1)S(1)} collective-permute-done((bf16[64,1792]{1,0:T(8,128)(2,1)S(1)}, bf16[64,1792]{1,0:T(8,128)(2,1)S(1)}, u32[]{:S(2)}, u32[]{:S(2)}) %collective-permute-start.20) | collective-permute-done | bytes 229408 | tf_op jit(solution)/shard_map/ppermute | solution.py:30
  130.1 3.3 %down.5.refs_3_ = bf16[1792,1024]{1,0:T(8,128)(2,1)S(1)} custom-call(bf16[1792,256]{1,0:T(8,128)(2,1)} %collective-permute-done.22.b_ref.refs_0_, bf16[1792,256]{1,0:T(8,128)(2,1)S(1)} %collective-permute-done.29.refs_1_, bf16[1024,1024]{1,0:T(8,128)(2,1)S(1)} %arrange.1.refs_2_, bf16[1792,1024]{1,0:T(8,128)(2,1)S(1)} %down.4.refs_3_), custom_call_target="tpu_custom_call" | custom-call | tf_op jit(solution)/shard_map/down/pallas_call | solution.py:375
  133.3 3.3 %down.6.refs_3_ = bf16[1792,1024]{1,0:T(8,128)(2,1)S(1)} custom-call(bf16[1792,256]{1,0:T(8,128)(2,1)} %collective-permute-done.21.a_ref.refs_0_, bf16[1792,256]{1,0:T(8,128)(2,1)S(1)} %collective-permute-done.28.refs_1_, bf16[1024,2048]{1,0:T(8,128)(2,1)S(1)} %copy-done.1, bf16[1792,1024]{1,0:T(8,128)(2,1)S(1)} %down.5.refs_3_), custom_call_target="tpu_custom_call" | custom-call | tf_op jit(solution)/shard_map/down/pallas_call | solution.py:375
  136.6 4.3 %down.7 = f32[1792,1024]{1,0:T(8,128)} custom-call(bf16[1792,256]{1,0:T(8,128)(2,1)S(1)} %collective-permute-done.23.refs_0_, bf16[1792,256]{1,0:T(8,128)(2,1)S(1)} %collective-permute-done.24.refs_1_, bf16[1024,1024]{1,0:T(8,128)(2,1)S(1)} %arrange.1.refs_2_, bf16[1792,1024]{1,0:T(8,128)(2,1)S(1)} %down.6.refs_3_), custom_call_target="tpu_custom_call" | custom-call | tf_op jit(solution)/shard_map/down/pallas_call | solution.py:375
  (81 shorter events, 29.1 us)
Async XLA Ops:
  9.5 10.9 %collective-permute-start.1 = (bf16[256,1024]{1,0:T(8,128)(2,1)S(1)}, bf16[256,1024]{1,0:T(8,128)(2,1)S(1)}, u32[]{:S(2)}, u32[]{:S(2)}) collective-permute-start(bf16[256,1024]{1,0:T(8,128)(2,1)S(1)} %get-tuple-element.38), channel_id=1, source_target_pairs={{0,2},{1,3},{2,0},{3,1},{4,6},{5,7},{6,4},{7,5},{8,10},{9,11},{10,... | collective-permute-start | bytes 1572872 | tf_op jit(solution)/shard_map/ppermute | solution.py:30
  14.2 8.2 %collective-permute-start.6 = (bf16[256,768]{1,0:T(8,128)(2,1)S(1)}, bf16[256,768]{1,0:T(8,128)(2,1)S(1)}, u32[]{:S(2)}, u32[]{:S(2)}) collective-permute-start(bf16[256,768]{1,0:T(8,128)(2,1)S(1)} %get-tuple-element.46), channel_id=1, source_target_pairs={{0,2},{1,3},{2,0},{3,1},{4,6},{5,7},{6,4},{7,5},{8,10},{9,11},{10,... | collective-permute-start | bytes 1179656 | tf_op jit(solution)/shard_map/ppermute | solution.py:30
  15.0 53.6 %collective-permute-start.22 = (bf16[1792,256]{1,0:T(8,128)(2,1)S(1)}, bf16[1792,256]{1,0:T(8,128)(2,1)}, u32[]{:S(2)}, u32[]{:S(2)}) collective-permute-start(bf16[1792,256]{1,0:T(8,128)(2,1)S(1)} %dequant.1.refs_0_), channel_id=1, source_target_pairs={{0,5},{1,4},{2,7},{3,6},{4,1},{5,0},{6,3},{7,2},{8,13},{9,12},{10,... | collective-permute-start | bytes 2752520 | tf_op jit(solution)/shard_map/ppermute | solution.py:30
  19.4 51.7 %collective-permute-start.21 = (bf16[1792,256]{1,0:T(8,128)(2,1)S(1)}, bf16[1792,256]{1,0:T(8,128)(2,1)}, u32[]{:S(2)}, u32[]{:S(2)}) collective-permute-start(bf16[1792,256]{1,0:T(8,128)(2,1)S(1)} %dequant.1.refs_0_), channel_id=1, source_target_pairs={{0,4},{1,5},{2,6},{3,7},{4,0},{5,1},{6,2},{7,3},{8,12},{9,13},{10,... | collective-permute-start | bytes 2752520 | tf_op jit(solution)/shard_map/ppermute | solution.py:30
  19.4 35.2 %collective-permute-start = (bf16[256,1024]{1,0:T(8,128)(2,1)}, bf16[256,1024]{1,0:T(8,128)(2,1)}, u32[]{:S(2)}, u32[]{:S(2)}) collective-permute-start(bf16[256,1024]{1,0:T(8,128)(2,1)} %get-tuple-element.36), channel_id=1, source_target_pairs={{0,2},{1,3},{2,0},{3,1},{4,6},{5,7},{6,4},{7,5},{8,10},{9,11},{10,... | collective-permute-start | bytes 1572872 | tf_op jit(solution)/shard_map/ppermute | solution.py:30
  20.4 30.7 %collective-permute-start.8 = (bf16[256,768]{1,0:T(8,128)(2,1)}, bf16[256,768]{1,0:T(8,128)(2,1)}, u32[]{:S(2)}, u32[]{:S(2)}) collective-permute-start(bf16[256,768]{1,0:T(8,128)(2,1)} %shard_map.86), channel_id=1, source_target_pairs={{0,4},{1,5},{2,6},{3,7},{4,0},{5,1},{6,2},{7,3},{8,12},{9,13},{10,... | collective-permute-start | bytes 1179656 | tf_op jit(solution)/shard_map/ppermute | solution.py:30
  23.2 40.6 %collective-permute-start.2 = (bf16[256,1024]{1,0:T(8,128)(2,1)S(1)}, bf16[256,1024]{1,0:T(8,128)(2,1)}, u32[]{:S(2)}, u32[]{:S(2)}) collective-permute-start(bf16[256,1024]{1,0:T(8,128)(2,1)S(1)} %shard_map.85), channel_id=1, source_target_pairs={{0,4},{1,5},{2,6},{3,7},{4,0},{5,1},{6,2},{7,3},{8,12},{9,13},{10,... | collective-permute-start | bytes 1572872 | tf_op jit(solution)/shard_map/ppermute | solution.py:30
  51.1 26.6 %collective-permute-start.25 = (bf16[256,1024]{1,0:T(8,128)(2,1)S(1)}, bf16[256,1024]{1,0:T(8,128)(2,1)S(1)}, u32[]{:S(2)}, u32[]{:S(2)}) collective-permute-start(bf16[256,1024]{1,0:T(8,128)(2,1)S(1)} %shard_map.91), channel_id=1, source_target_pairs={{0,1},{1,0},{2,3},{3,2},{4,5},{5,4},{6,7},{7,6},{8,9},{9,8},{10,11... | collective-permute-start | bytes 1572872 | tf_op jit(solution)/shard_map/ppermute | solution.py:30
  63.8 9.5 %collective-permute-start.9 = (bf16[64,768]{1,0:T(8,128)(2,1)S(1)}, bf16[64,768]{1,0:T(8,128)(2,1)S(1)}, u32[]{:S(2)}, u32[]{:S(2)}) collective-permute-start(bf16[64,768]{1,0:T(8,128)(2,1)S(1)} %get-tuple-element.50), channel_id=1, source_target_pairs={{0,8},{1,9},{2,34},{3,35},{4,12},{5,13},{6,38},{7,39},{8,0},{9,1},... | collective-permute-start | bytes 294920 | tf_op jit(solution)/shard_map/ppermute | solution.py:30
  66.7 9.2 %collective-permute-start.3 = (bf16[64,1024]{1,0:T(8,128)(2,1)S(1)}, bf16[64,1024]{1,0:T(8,128)(2,1)S(1)}, u32[]{:S(2)}, u32[]{:S(2)}) collective-permute-start(bf16[64,1024]{1,0:T(8,128)(2,1)S(1)} %get-tuple-element.40), channel_id=1, source_target_pairs={{0,8},{1,9},{2,34},{3,35},{4,12},{5,13},{6,38},{7,39},{8,0},{9,1},... | collective-permute-start | bytes 393224 | tf_op jit(solution)/shard_map/ppermute | solution.py:30
  68.6 7.3 %collective-permute-start.4 = (bf16[64,1024]{1,0:T(8,128)(2,1)S(1)}, bf16[64,1024]{1,0:T(8,128)(2,1)S(1)}, u32[]{:S(2)}, u32[]{:S(2)}) collective-permute-start(bf16[64,1024]{1,0:T(8,128)(2,1)S(1)} %get-tuple-element.41), channel_id=1, source_target_pairs={{0,16},{1,17},{2,66},{3,67},{4,20},{5,21},{6,70},{7,71},{8,24},{9,... | collective-permute-start | bytes 393224 | tf_op jit(solution)/shard_map/ppermute | solution.py:30
  73.2 33.2 %collective-permute-start.23 = (bf16[1792,256]{1,0:T(8,128)(2,1)S(1)}, bf16[1792,256]{1,0:T(8,128)(2,1)S(1)}, u32[]{:S(2)}, u32[]{:S(2)}) collective-permute-start(bf16[1792,256]{1,0:T(8,128)(2,1)S(1)} %shard_map.90), channel_id=1, source_target_pairs={{0,5},{1,4},{2,6},{3,7},{4,1},{5,0},{6,2},{7,3},{8,13},{9,12},{10,... | collective-permute-start | bytes 2752520 | tf_op jit(solution)/shard_map/ppermute | solution.py:30
  77.7 19.8 %collective-permute-start.26 = (bf16[256,1024]{1,0:T(8,128)(2,1)S(1)}, bf16[256,1024]{1,0:T(8,128)(2,1)S(1)}, u32[]{:S(2)}, u32[]{:S(2)}) collective-permute-start(bf16[256,1024]{1,0:T(8,128)(2,1)S(1)} %collective-permute-done.25.a_ref.g0), channel_id=1, source_target_pairs={{0,24},{1,25},{2,98},{3,99},{4,28},{5,29},{6,102},{7,103},{8,16},{... | collective-permute-start | bytes 1572872 | tf_op jit(solution)/shard_map/ppermute | solution.py:30
  79.6 27.7 %collective-permute-start.30 = (bf16[1792,256]{1,0:T(8,128)(2,1)S(1)}, bf16[1792,256]{1,0:T(8,128)(2,1)S(1)}, u32[]{:S(2)}, u32[]{:S(2)}) collective-permute-start(bf16[1792,256]{1,0:T(8,128)(2,1)S(1)} %dequant.1.refs_0_), channel_id=1, source_target_pairs={{0,2},{1,3},{2,0},{3,1},{4,6},{5,7},{6,4},{7,5},{8,10},{9,11},{10,... | collective-permute-start | bytes 2752520 | tf_op jit(solution)/shard_map/ppermute | solution.py:30
  79.6 7.6 %collective-permute-start.13 = (bf16[64,1792]{1,0:T(8,128)(2,1)S(1)}, bf16[64,1792]{1,0:T(8,128)(2,1)S(1)}, u32[]{:S(2)}, u32[]{:S(2)}) collective-permute-start(bf16[64,1792]{1,0:T(8,128)(2,1)S(1)} %get-tuple-element.55), channel_id=1, source_target_pairs={{0,16},{1,17},{2,66},{3,67},{4,20},{5,21},{6,70},{7,71},{8,24},{9,... | collective-permute-start | bytes 688136 | tf_op jit(solution)/shard_map/ppermute | solution.py:30
  83.7 9.4 %collective-permute-start.14 = (bf16[64,1792]{1,0:T(8,128)(2,1)S(1)}, bf16[64,1792]{1,0:T(8,128)(2,1)S(1)}, u32[]{:S(2)}, u32[]{:S(2)}) collective-permute-start(bf16[64,1792]{1,0:T(8,128)(2,1)S(1)} %get-tuple-element.56), channel_id=1, source_target_pairs={{0,24},{1,25},{2,98},{3,99},{4,28},{5,29},{6,102},{7,103},{8,16},{... | collective-permute-start | bytes 688136 | tf_op jit(solution)/shard_map/ppermute | solution.py:30
  94.8 9.3 %collective-permute-start.16 = (bf16[64,1792]{1,0:T(8,128)(2,1)S(1)}, bf16[64,1792]{1,0:T(8,128)(2,1)S(1)}, u32[]{:S(2)}, u32[]{:S(2)}) collective-permute-start(bf16[64,1792]{1,0:T(8,128)(2,1)S(1)} %get-tuple-element.59), channel_id=1, source_target_pairs={{0,64},{1,65},{2,18},{3,19},{4,68},{5,69},{6,22},{7,23},{8,72},{9,... | collective-permute-start | bytes 688136 | tf_op jit(solution)/shard_map/ppermute | solution.py:30
  97.5 8.9 %collective-permute-start.17 = (bf16[64,1792]{1,0:T(8,128)(2,1)S(1)}, bf16[64,1792]{1,0:T(8,128)(2,1)S(1)}, u32[]{:S(2)}, u32[]{:S(2)}) collective-permute-start(bf16[64,1792]{1,0:T(8,128)(2,1)S(1)} %get-tuple-element.60), channel_id=1, source_target_pairs={{0,96},{1,97},{2,26},{3,27},{4,100},{5,101},{6,30},{7,31},{8,104},... | collective-permute-start | bytes 688136 | tf_op jit(solution)/shard_map/ppermute | solution.py:30
  99.3 30.6 %collective-permute-start.27 = (bf16[2,256,1024]{2,1,0:T(8,128)(2,1)S(1)}, bf16[2,256,1024]{2,1,0:T(8,128)(2,1)S(1)}, u32[]{:S(2)}, u32[]{:S(2)}) collective-permute-start(bf16[2,256,1024]{2,1,0:T(8,128)(2,1)S(1)} %shard_map.92), channel_id=1, source_target_pairs={{0,96},{1,97},{2,26},{3,27},{4,100},{5,101},{6,30},{7,31},{8,104},... | collective-permute-start | bytes 3145736 | tf_op jit(solution)/shard_map/ppermute | solution.py:30
  104.0 26.0 %collective-permute-start.29 = (bf16[1792,256]{1,0:T(8,128)(2,1)}, bf16[1792,256]{1,0:T(8,128)(2,1)S(1)}, u32[]{:S(2)}, u32[]{:S(2)}) collective-permute-start(bf16[1792,256]{1,0:T(8,128)(2,1)} %collective-permute-done.22.b_ref.refs_0_), channel_id=1, source_target_pairs={{0,2},{1,3},{2,0},{3,1},{4,6},{5,7},{6,4},{7,5},{8,10},{9,11},{10,... | collective-permute-start | bytes 2752520 | tf_op jit(solution)/shard_map/ppermute | solution.py:30
  106.4 26.9 %collective-permute-start.28 = (bf16[1792,256]{1,0:T(8,128)(2,1)}, bf16[1792,256]{1,0:T(8,128)(2,1)S(1)}, u32[]{:S(2)}, u32[]{:S(2)}) collective-permute-start(bf16[1792,256]{1,0:T(8,128)(2,1)} %collective-permute-done.21.a_ref.refs_0_), channel_id=1, source_target_pairs={{0,2},{1,3},{2,0},{3,1},{4,6},{5,7},{6,4},{7,5},{8,10},{9,11},{10,... | collective-permute-start | bytes 2752520 | tf_op jit(solution)/shard_map/ppermute | solution.py:30
  106.4 30.2 %collective-permute-start.24 = (bf16[1792,256]{1,0:T(8,128)(2,1)S(1)}, bf16[1792,256]{1,0:T(8,128)(2,1)S(1)}, u32[]{:S(2)}, u32[]{:S(2)}) collective-permute-start(bf16[1792,256]{1,0:T(8,128)(2,1)S(1)} %collective-permute-done.23.refs_0_), channel_id=1, source_target_pairs={{0,2},{1,3},{2,0},{3,1},{4,6},{5,7},{6,4},{7,5},{8,10},{9,11},{10,... | collective-permute-start | bytes 2752520 | tf_op jit(solution)/shard_map/ppermute | solution.py:30
  113.4 7.5 %collective-permute-start.19 = (bf16[64,1792]{1,0:T(8,128)(2,1)S(1)}, bf16[64,1792]{1,0:T(8,128)(2,1)S(1)}, u32[]{:S(2)}, u32[]{:S(2)}) collective-permute-start(bf16[64,1792]{1,0:T(8,128)(2,1)S(1)} %get-tuple-element.63), channel_id=1, source_target_pairs={{0,64},{1,65},{2,18},{3,19},{4,68},{5,69},{6,22},{7,23},{8,72},{9,... | collective-permute-start | bytes 688136 | tf_op jit(solution)/shard_map/ppermute | solution.py:30
  120.9 7.2 %collective-permute-start.20 = (bf16[64,1792]{1,0:T(8,128)(2,1)S(1)}, bf16[64,1792]{1,0:T(8,128)(2,1)S(1)}, u32[]{:S(2)}, u32[]{:S(2)}) collective-permute-start(bf16[64,1792]{1,0:T(8,128)(2,1)S(1)} %get-tuple-element.64), channel_id=1, source_target_pairs={{0,96},{1,97},{2,26},{3,27},{4,100},{5,101},{6,30},{7,31},{8,104},... | collective-permute-start | bytes 688136 | tf_op jit(solution)/shard_map/ppermute | solution.py:30
  (19 other events, 137.5 us)
